TPU v7x, 256 devices: a whole 4x4x8 slice. The times are simulated.
256 devices in a mesh: col: 64 (over z, x, core), row: 4 (over y).
Axes of the slice: x: 4, y: 4, z: 8, core: 2. Of those that a mesh axis runs over, the one named last changes fastest.
Arguments:
- matrix: float32 [16, 512, 1, 8192], P(None, 'row', None, 'col'), may hold values from -1 to 5, as said below
- inverse_factors: float32 [2, 512, 512], replicated, may hold values from -1 to 1, as said below
Outputs:
- factored: float32 [16, 512, 1, 8192], P(None, 'row', None, 'col')
Inputs may be any that keep to these rules, and one draw needn't show every extreme that they name: matrix holds a symmetric matrix. Each inverse_factors[k] is lower triangular with a positive diagonal; it is given independently of matrix.
All inputs are finite; a program needn't handle non-finite values.
Results may differ from a plain program's by a relative error of at most 0.0001.
Values sent between devices are 32-bit elements; how exact they have to be, the bound alone decides.
No kernel may reach another device: no remote copies, remote signals or barrier semaphores. Data moves between devices by JAX's collectives and lax.ppermute only.
A program may use at most 64 MiB of HBM per device.

v0:
```python
import jax
import jax.numpy as jnp
from jax import lax
from jax.experimental import pallas as pl
from jax.experimental.pallas import tpu as pltpu
from jax.sharding import Mesh
from jax.sharding import PartitionSpec as P

Z, X, K, Y = 8, 4, 2, 4
B = 128
FIRST = (0, 2, 1, 3)
SECOND = (1, 3, 0, 2)


def shift(v, axis, size, step):
    return lax.ppermute(v, axis, [(i, (i + step) % size) for i in range(size)])


def other_core(v):
    return lax.ppermute(v, "k", [(0, 1), (1, 0)])


def swap(v, choice):
    perm = []
    for x in range(X):
        for k in range(K):
            for y in range(Y):
                source = ((2 * k + (y >> 1)) * K + (y & 1)) * Y + choice[x]
                perm.append((source, (x * K + k) * Y + y))
    return lax.ppermute(v, ("x", "k", "y"), perm)


def after(value, *done):
    return lax.optimization_barrier((value, *done))[0]


def after2(values, *done):
    return lax.optimization_barrier((*values, *done))[: len(values)]


def gather_y(v):
    return [v] + [shift(v, "y", Y, s) for s in range(1, Y)]


def split(v):
    high = v.astype(jnp.bfloat16)
    return high, (v - high.astype(jnp.float32)).astype(jnp.bfloat16)


def mul(a, b, transposed):
    dims = (((1,), (1 if transposed else 0,)), ((), ()))
    f = lambda u, v: lax.dot_general(u, v, dims, preferred_element_type=jnp.float32)
    return f(a[0], b[0]) + (f(a[0], b[1]) + f(a[1], b[0]))


VMEM = pl.BlockSpec(memory_space=pltpu.VMEM)
SMEM = pl.BlockSpec(memory_space=pltpu.SMEM)


def at_block(i, n=1):
    return pl.ds(pl.multiple_of(i * B, B), n * B)


def factor(pos, inverse, mine, theirs, corner):
    def body(pos_ref, l_ref, m0, m1, m2, m3, th, c0, c1, c2, c3, fh, fl, ah, al, xc, gs, zz, vv):
        z, x, k, y = (pos_ref[i] for i in range(4))
        low = x < 2
        for s, (m, c) in enumerate(zip((m0, m1, m2, m3), (c0, c1, c2, c3))):
            from_y = lax.rem(y + (Y - s), Y)
            for p in range(2):
                lanes = at_block(4 * p + from_y)
                xc[:B, lanes] = m[p]
                xc[B:, lanes] = th[s, p]
            for i in range(4):
                gs[at_block(jnp.where(low, i, from_y)), at_block(jnp.where(low, from_y, i))] = c[i]
        l0, l1, g = split(l_ref[0]), split(l_ref[1]), split(gs[...])
        row = lax.broadcasted_iota(jnp.int32, (2 * B, 4 * B), 0)
        col = lax.broadcasted_iota(jnp.int32, (2 * B, 4 * B), 1)
        block = 2 * (x & 1) + jnp.where(row < B, k, 1 - k)
        unit = jnp.where(col == block * B + (row & (B - 1)), 1.0, 0.0)
        w = mul(split(xc[:, : 4 * B]), l0, True)
        v = mul(split(w), l0, False)
        u = mul(split(xc[:, 4 * B :] - mul(split(v), g, False)), l1, True)
        corner_slab = z == 0
        w = jnp.where(corner_slab, jnp.where(low, unit, 0.0), w)
        u = jnp.where(corner_slab, jnp.where(low, 0.0, unit), u)
        zb = mul(split(u), l1, False)
        zt = mul(split(w - mul(split(mul(split(zb), g, True)), l0, True)), l0, False)
        sign = jnp.where(corner_slab, -1.0, 1.0)
        zz[:, : 4 * B] = zt * sign
        zz[:, 4 * B :] = zb * sign
        vv[:, : 4 * B] = jnp.where(
            corner_slab,
            jnp.where((k == 1) | low, zt * sign, 0.0),
            jnp.where(k == 1, v, 0.0),
        )
        vv[:, 4 * B :] = jnp.where(corner_slab & ((k == 1) | low), zb * sign, 0.0)
        pick = lambda table, i: jnp.where(i == 0, table[0], jnp.where(i == 1, table[1], jnp.where(i == 2, table[2], table[3])))
        which = (pick(FIRST, x), pick(SECOND, x), pick(FIRST, (x + 3) & 3), pick(FIRST, (x + 1) & 3))
        for p in range(2):
            for j in range(4):
                lanes = slice((4 * p + j) * B, (4 * p + j + 1) * B)
                fh[:, lanes], fl[:, lanes] = split(zz[:, at_block(4 * p + which[j])])
                ah[:, lanes], al[:, lanes] = split(vv[:, at_block(4 * p + which[j])])

    half = jax.ShapeDtypeStruct((2 * B, 8 * B), jnp.bfloat16)
    return pl.pallas_call(
        body,
        out_shape=(half,) * 4,
        in_specs=[SMEM] + [VMEM] * 10,
        out_specs=(VMEM,) * 4,
        scratch_shapes=[
            pltpu.VMEM((2 * B, 8 * B), jnp.float32),
            pltpu.VMEM((4 * B, 4 * B), jnp.float32),
            pltpu.VMEM((2 * B, 8 * B), jnp.float32),
            pltpu.VMEM((2 * B, 8 * B), jnp.float32),
        ],
        compiler_params=pltpu.CompilerParams(vmem_limit_bytes=32 * 2**20),
        cost_estimate=pl.CostEstimate(flops=8 * 3 * 2 * 512 * 512 * 256, bytes_accessed=6 * 2**20, transcendentals=0),
        name="factor",
    )(pos, inverse, *mine, theirs, *corner)


def product(pos, pieces, zs):
    names = [(t, c) for t in range(Z) for c in range(8)]
    arrays, index = [], {}
    for name in names:
        array, at = pieces[name]
        for i, known in enumerate(arrays):
            if known is array:
                break
        else:
            i = len(arrays)
            arrays.append(array)
        index[name] = (i, at)

    def body(pos_ref, *refs):
        xs = refs[: len(arrays)]
        zh, zl, yh, yl, own, oth, xh, xl = refs[len(arrays) :]
        for t, c in names:
            i, at = index[(t, c)]
            high, low = split(xs[i][at])
            xh[t * B : (t + 1) * B, c * B : (c + 1) * B] = high
            xl[t * B : (t + 1) * B, c * B : (c + 1) * B] = low
        z = pos_ref[0]
        res = mul((xh[...], xl[...]), (zh[...], zl[...]), True)
        for t in range(Z):
            rows = at_block(lax.rem(z + t, Z))
            own[rows, :] = res[t * B : (t + 1) * B, :B]
            oth[rows, :] = res[t * B : (t + 1) * B, B:]
        rows = at_block(lax.rem(Z - z, Z))
        alt = mul((xh[rows, :], xl[rows, :]), (yh[...], yl[...]), True)
        own[:B, :] = alt[:, :B]
        oth[:B, :] = alt[:, B:]

    half = jax.ShapeDtypeStruct((Z * B, B), jnp.float32)
    return pl.pallas_call(
        body,
        out_shape=(half, half),
        in_specs=[SMEM] + [VMEM] * (len(arrays) + 4),
        out_specs=(VMEM, VMEM),
        scratch_shapes=[pltpu.VMEM((Z * B, 8 * B), jnp.bfloat16)] * 2,
        compiler_params=pltpu.CompilerParams(vmem_limit_bytes=32 * 2**20),
        cost_estimate=pl.CostEstimate(flops=2 * 3 * 1024 * 1024 * 256, bytes_accessed=7 * 2**20, transcendentals=0),
        name="product",
    )(pos, *arrays, *zs)


def finish(pos, a, own, got):
    def body(pos_ref, a_ref, own_ref, got_ref, out_ref):
        z, k = pos_ref[0], pos_ref[2]
        for t in range(Z):
            out_ref[2 * t + k] = jnp.where(z == 0, 0.0, a_ref[2 * t + k]) - own_ref[t]
            out_ref[2 * t + 1 - k] = jnp.where(z == 0, 0.0, a_ref[2 * t + 1 - k]) - got_ref[t]

    return pl.pallas_call(
        body,
        out_shape=jax.ShapeDtypeStruct((2 * Z, B, B), jnp.float32),
        in_specs=[SMEM] + [VMEM] * 3,
        out_specs=VMEM,
        compiler_params=pltpu.CompilerParams(vmem_limit_bytes=16 * 2**20),
        cost_estimate=pl.CostEstimate(flops=2**18, bytes_accessed=3 * 2**20, transcendentals=0),
        name="finish",
    )(pos, a, own.reshape(Z, B, B), got.reshape(Z, B, B))


def shards(matrix, inverse_factors):
    z, x, k, y = (lax.axis_index(n) for n in ("z", "x", "k", "y"))
    pos = jnp.stack([z, x, k, y]).astype(jnp.int32)
    a = matrix.reshape(16, B, B)

    blocks = jnp.swapaxes(a[:2], 1, 2)
    f0, g0 = swap(blocks, FIRST), swap(blocks, SECOND)

    def step(u, d):
        return shift(u, "z", Z, 1), shift(d, "z", Z, -1)

    def last(u, d):
        return shift(u[:1], "z", Z, 1), shift(d[1:], "z", Z, -1)

    def along_x(*parts):
        v = jnp.concatenate(parts)
        return shift(v, "x", X, 1), shift(v, "x", X, -1)

    corner = jnp.where(x < 2, blocks[1], a[0])

    def spread(v, reach):
        got = lax.ppermute(v, "z", [(i, i + reach) for i in range(0, Z, 2 * reach)])
        return jnp.where(z % (2 * reach) == reach, got, v)

    corner = spread(corner, 4)
    f1u, f1d = step(f0, f0)
    g1u, g1d = step(g0, g0)
    corner = spread(after(corner, f0), 2)
    rows = gather_y(after(blocks, f0))
    f2u, f2d = step(*after2((f1u, f1d), corner))
    x0 = along_x(f0, f1u, f1d)
    corner = spread(corner, 1)
    g2u, g2d = step(g1u, g1d)
    f3u, f3d = step(*after2((f2u, f2d), corner))
    got = other_core(corner)
    corner = jnp.stack([jnp.where(k == 0, corner, got), jnp.where(k == 0, got, corner)])
    got = lax.ppermute(corner, "x", [(0, 1), (1, 0), (2, 3), (3, 2)])
    corner = jnp.stack([jnp.where(x % 2 == 0, corner, got), jnp.where(x % 2 == 0, got, corner)]).reshape(4, B, B)
    x1 = along_x(*after2((f2u, f2d), *x0))
    g3u, g3d = step(*after2((g2u, g2d), *x0))
    fa, fb = last(*after2((f3u, f3d), corner))
    corners = gather_y(corner)
    ga, gb = last(*after2((g3u, g3d), *x1))
    x2 = along_x(f3u, f3d, fa, fb)
    theirs = other_core(jnp.stack(rows))

    pieces = {}
    first = {0: f0, 1: f1d, 2: f2d, 3: f3d, 5: f3u, 6: f2u, 7: f1u}
    second = {0: g0, 1: g1d, 2: g2d, 3: g3d, 5: g3u, 6: g2u, 7: g1u}
    beside = {0: (x0, 0), 7: (x0, 2), 1: (x0, 4), 6: (x1, 0), 2: (x1, 2), 5: (x2, 0), 3: (x2, 2), 4: (x2, 4)}
    for t in range(Z):
        for p in range(2):
            pieces[(t, 4 * p)] = ((fa, fb)[p], 0) if t == 4 else (first[t], p)
            pieces[(t, 4 * p + 1)] = ((ga, gb)[p], 0) if t == 4 else (second[t], p)
            arrived, at = beside[t]
            pieces[(t, 4 * p + 2)] = (arrived[0], at + p)
            pieces[(t, 4 * p + 3)] = (arrived[1], at + p)

    zs = factor(pos, inverse_factors, rows, theirs, corners)
    own, other = product(pos, pieces, zs)
    return finish(pos, a, own, other_core(other)).reshape(16, B, 1, B)


def solution(mesh):
    fine = Mesh(mesh.devices.reshape(Z, X, K, Y), ("z", "x", "k", "y"))
    spec = P(None, "y", None, ("z", "x", "k"))
    return jax.shard_map(shards, mesh=fine, in_specs=(spec, P()), out_specs=spec, check_vma=False)
```

profile of v0, /device:TPU:1, one launch (start us, length us, event | category | flops | bytes accessed | tf_op | source)
XLA Modules:
  0.0 107.2 jit_solution(17904712284129986635)
XLA Ops:
  0.0 0.9 slice.25
  0.9 0.1 copy.6
  1.0 0.9 fusion
  1.9 9.6 %collective-permute-start.7 = (f32[128,128]{1,0:T(8,128)S(1)}, f32[128,128]{1,0:T(8,128)S(1)}, u32[]{:S(2)}, u32[]{:S(2)}) collective-permute-start(f32[128,128]{1,0:T(8,128)S(1)} %fusion), channel_id=1, source_target_pairs={{0,128},{1,129},{2,130},{3,131},{4,132},{5,133},{6,134},{7,135},{8... | collective-permute-start | bytes 196616 | tf_op jit(solution)/shard_map/ppermute | solution.py:208
  11.5 4.0 %collective-permute-start = (f32[2,128,128]{2,1,0:T(8,128)S(1)}, f32[2,128,128]{2,1,0:T(8,128)S(1)}, u32[]{:S(2)}, u32[]{:S(2)}) collective-permute-start(f32[2,128,128]{2,1,0:T(8,128)S(1)} %bitcast.38), channel_id=1, source_target_pairs={{0,0},{4,1},{8,2},{12,3},{16,4},{20,5},{24,6},{28,7},{2,8},{6,9},{... | collective-permute-start | bytes 393224 | tf_op jit(solution)/shard_map/ppermute | solution.py:30
  15.6 0.0 collective-permute-done.7
  15.6 5.5 %collective-permute-done.refs_0_ = f32[2,128,128]{2,1,0:T(8,128)S(1)} collective-permute-done((f32[2,128,128]{2,1,0:T(8,128)S(1)}, f32[2,128,128]{2,1,0:T(8,128)S(1)}, u32[]{:S(2)}, u32[]{:S(2)}) %collective-permute-start) | collective-permute-done | bytes 131104 | tf_op jit(solution)/shard_map/ppermute | solution.py:30
  21.1 1.3 %collective-permute-start.8 = (f32[128,128]{1,0:T(8,128)S(1)}, f32[128,128]{1,0:T(8,128)S(1)}, u32[]{:S(2)}, u32[]{:S(2)}) collective-permute-start(f32[128,128]{1,0:T(8,128)S(1)} %broadcast_select_fusion.1), channel_id=1, source_target_pairs={{0,64},{128,192},{1,65},{129,193},{2,66},{130,194},{3,67},{131,195... | collective-permute-start | bytes 196616 | tf_op jit(solution)/shard_map/ppermute | solution.py:208
  22.4 4.0 %collective-permute-start.1 = (f32[2,128,128]{2,1,0:T(8,128)S(1)}, f32[2,128,128]{2,1,0:T(8,128)S(1)}, u32[]{:S(2)}, u32[]{:S(2)}) collective-permute-start(f32[2,128,128]{2,1,0:T(8,128)S(1)} %bitcast.39), channel_id=1, source_target_pairs={{1,0},{5,1},{9,2},{13,3},{17,4},{21,5},{25,6},{29,7},{3,8},{7,9},{... | collective-permute-start | bytes 393224 | tf_op jit(solution)/shard_map/ppermute | solution.py:30
  26.4 0.0 collective-permute-start.29
  26.4 6.5 %collective-permute-start.30 = (f32[2,128,128]{2,1,0:T(8,128)S(1)}, f32[2,128,128]{2,1,0:T(8,128)S(1)}, u32[]{:S(2)}, u32[]{:S(2)}) collective-permute-start(f32[2,128,128]{2,1,0:T(8,128)S(1)} %bitcast.41), channel_id=1, source_target_pairs={{0,2},{1,3},{2,0},{3,1},{4,6},{5,7},{6,4},{7,5},{8,10},{9,11},{10,... | collective-permute-start | bytes 393224 | tf_op jit(solution)/shard_map/ppermute | solution.py:16
  32.9 0.0 collective-permute-start.2
  32.9 0.0 collective-permute-done.8
  32.9 1.3 %collective-permute-start.14 = (f32[128,128]{1,0:T(8,128)S(1)}, f32[128,128]{1,0:T(8,128)S(1)}, u32[]{:S(2)}, u32[]{:S(2)}) collective-permute-start(f32[128,128]{1,0:T(8,128)S(1)} %broadcast_select_fusion.2), channel_id=1, source_target_pairs={{0,32},{64,96},{128,160},{192,224},{1,33},{65,97},{129,161},{193,2... | collective-permute-start | bytes 196616 | tf_op jit(solution)/shard_map/ppermute | solution.py:208
  34.2 2.2 %collective-permute-done.14 = f32[128,128]{1,0:T(8,128)S(1)} collective-permute-done((f32[128,128]{1,0:T(8,128)S(1)}, f32[128,128]{1,0:T(8,128)S(1)}, u32[]{:S(2)}, u32[]{:S(2)}) %collective-permute-start.14) | collective-permute-done | bytes 65568 | tf_op jit(solution)/shard_map/ppermute | solution.py:208
  36.4 4.1 %collective-permute-start.3 = (f32[2,128,128]{2,1,0:T(8,128)S(1)}, f32[2,128,128]{2,1,0:T(8,128)S(1)}, u32[]{:S(2)}, u32[]{:S(2)}) collective-permute-start(f32[2,128,128]{2,1,0:T(8,128)S(1)} %collective-permute-done.refs_0_), channel_id=1, source_target_pairs={{0,224},{32,0},{64,32},{96,64},{128,96},{160,128},{192,160},{224,1... | collective-permute-start | bytes 393224 | tf_op jit(solution)/shard_map/ppermute | solution.py:16
  40.6 0.0 collective-permute-done.1.refs_1_
  40.6 2.1 %collective-permute-start.31 = (f32[2,128,128]{2,1,0:T(8,128)S(1)}, f32[2,128,128]{2,1,0:T(8,128)S(1)}, u32[]{:S(2)}, u32[]{:S(2)}) collective-permute-start(f32[2,128,128]{2,1,0:T(8,128)S(1)} %bitcast.42), channel_id=1, source_target_pairs={{0,3},{1,0},{2,1},{3,2},{4,7},{5,4},{6,5},{7,6},{8,11},{9,8},{10,9... | collective-permute-start | bytes 393224 | tf_op jit(solution)/shard_map/ppermute | solution.py:16
  42.7 0.0 collective-permute-start.6
  42.7 3.7 %collective-permute-start.20 = (f32[128,128]{1,0:T(8,128)S(1)}, f32[128,128]{1,0:T(8,128)S(1)}, u32[]{:S(2)}, u32[]{:S(2)}) collective-permute-start(f32[128,128]{1,0:T(8,128)S(1)} %broadcast_select_fusion), channel_id=1, source_target_pairs={{0,4},{4,0},{1,5},{5,1},{2,6},{6,2},{3,7},{7,3},{8,12},{12,8},{9,1... | collective-permute-start | bytes 196616 | tf_op jit(solution)/shard_map/ppermute | solution.py:20
  46.5 0.9 collective-permute-done.20
  47.4 1.3 %collective-permute-start.11 = (f32[2,128,128]{2,1,0:T(8,128)S(1)}, f32[2,128,128]{2,1,0:T(8,128)S(1)}, u32[]{:S(2)}, u32[]{:S(2)}) collective-permute-start(f32[2,128,128]{2,1,0:T(8,128)S(1)} %collective-permute-done.2.refs_22_), channel_id=1, source_target_pairs={{0,32},{32,64},{64,96},{96,128},{128,160},{160,192},{192,224},{224... | collective-permute-start | bytes 393224 | tf_op jit(solution)/shard_map/ppermute | solution.py:16
  48.6 0.0 copy-start.1
  48.7 0.0 collective-permute-done.29.m1
  48.7 2.2 %collective-permute-start.9 = (f32[2,128,128]{2,1,0:T(8,128)S(1)}, f32[2,128,128]{2,1,0:T(8,128)S(1)}, u32[]{:S(2)}, u32[]{:S(2)}) collective-permute-start(f32[2,128,128]{2,1,0:T(8,128)S(1)} %collective-permute-done.3.refs_4_), channel_id=1, source_target_pairs={{0,224},{32,0},{64,32},{96,64},{128,96},{160,128},{192,160},{224,1... | collective-permute-start | bytes 393224 | tf_op jit(solution)/shard_map/ppermute | solution.py:16
  50.9 0.0 collective-permute-start.21
  50.9 0.0 collective-permute-done.31.m3
  50.9 0.1 collective-permute-start.16
  51.1 3.3 %collective-permute-done.11.refs_20_ = f32[2,128,128]{2,1,0:T(8,128)S(1)} collective-permute-done((f32[2,128,128]{2,1,0:T(8,128)S(1)}, f32[2,128,128]{2,1,0:T(8,128)S(1)}, u32[]{:S(2)}, u32[]{:S(2)}) %collective-permute-start.11) | collective-permute-done | bytes 131104 | tf_op jit(solution)/shard_map/ppermute | solution.py:16
  54.4 0.0 collective-permute-start.4
  54.4 0.0 collective-permute-done.9.refs_6_
  54.4 2.7 %collective-permute-start.5 = (f32[6,128,128]{2,1,0:T(8,128)S(1)}, f32[6,128,128]{2,1,0:T(8,128)S(1)}, u32[]{:S(2)}, u32[]{:S(2)}) collective-permute-start(f32[6,128,128]{2,1,0:T(8,128)S(1)} %constant_dynamic-update-slice_fusion), channel_id=1, source_target_pairs={{0,24},{8,0},{16,8},{24,16},{1,25},{9,1},{17,9},{25,17},{2,26},{10... | collective-permute-start | bytes 1179656 | tf_op jit(solution)/shard_map/ppermute | solution.py:16
  57.0 0.0 collective-permute-done.6.refs_5_
  57.0 1.1 %collective-permute-start.15 = (f32[2,128,128]{2,1,0:T(8,128)S(1)}, f32[2,128,128]{2,1,0:T(8,128)S(1)}, u32[]{:S(2)}, u32[]{:S(2)}) collective-permute-start(f32[2,128,128]{2,1,0:T(8,128)S(1)} %collective-permute-done.9.refs_6_), channel_id=1, source_target_pairs={{0,224},{32,0},{64,32},{96,64},{128,96},{160,128},{192,160},{224,1... | collective-permute-start | bytes 393224 | tf_op jit(solution)/shard_map/ppermute | solution.py:16
  58.2 0.0 collective-permute-done.21
  58.2 0.3 collective-permute-start.19
  58.5 2.4 %collective-permute-start.10 = (f32[2,128,128]{2,1,0:T(8,128)S(1)}, f32[2,128,128]{2,1,0:T(8,128)S(1)}, u32[]{:S(2)}, u32[]{:S(2)}) collective-permute-start(f32[2,128,128]{2,1,0:T(8,128)S(1)} %collective-permute-done.6.refs_5_), channel_id=1, source_target_pairs={{0,224},{32,0},{64,32},{96,64},{128,96},{160,128},{192,160},{224,1... | collective-permute-start | bytes 393224 | tf_op jit(solution)/shard_map/ppermute | solution.py:16
  61.0 0.2 collective-permute-done.15.refs_10_
  61.1 0.0 collective-permute-start.17
  61.2 2.3 %collective-permute-done.19.refs_18_ = f32[2,128,128]{2,1,0:T(8,128)S(1)} collective-permute-done((f32[2,128,128]{2,1,0:T(8,128)S(1)}, f32[2,128,128]{2,1,0:T(8,128)S(1)}, u32[]{:S(2)}, u32[]{:S(2)}) %collective-permute-start.19) | collective-permute-done | bytes 131104 | tf_op jit(solution)/shard_map/ppermute | solution.py:16
  63.5 0.0 collective-permute-start.33
  63.6 1.8 %collective-permute-done.4.refs_2_ = f32[6,128,128]{2,1,0:T(8,128)S(1)} collective-permute-done((f32[6,128,128]{2,1,0:T(8,128)S(1)}, f32[6,128,128]{2,1,0:T(8,128)S(1)}, u32[]{:S(2)}, u32[]{:S(2)}) %collective-permute-start.4) | collective-permute-done | bytes 393248 | tf_op jit(solution)/shard_map/ppermute | solution.py:16
  65.3 3.1 %collective-permute-start.32 = (f32[4,2,128,128]{3,2,1,0:T(8,128)S(1)}, f32[4,2,128,128]{3,2,1,0:T(8,128)S(1)}, u32[]{:S(2)}, u32[]{:S(2)}) collective-permute-start(f32[4,2,128,128]{3,2,1,0:T(8,128)S(1)} %pad_maximum_fusion), channel_id=1, source_target_pairs={{0,4},{4,0},{1,5},{5,1},{2,6},{6,2},{3,7},{7,3},{8,12},{12,8},{9,1... | collective-permute-start | bytes 1572872 | tf_op jit(solution)/shard_map/ppermute | solution.py:20
  68.4 0.0 collective-permute-done.5.refs_3_
  68.4 0.0 collective-permute-start.22
  68.4 2.7 %collective-permute-start.23 = (f32[1,128,128]{2,1,0:T(8,128)S(1)}, f32[1,128,128]{2,1,0:T(8,128)S(1)}, u32[]{:S(2)}, u32[]{:S(2)}) collective-permute-start(f32[1,128,128]{2,1,0:T(8,128)S(1)} %slice.30), channel_id=1, source_target_pairs={{0,224},{32,0},{64,32},{96,64},{128,96},{160,128},{192,160},{224,1... | collective-permute-start | bytes 196616 | tf_op jit(solution)/shard_map/ppermute | solution.py:16
  71.1 0.1 collective-permute-start.18
  71.2 2.1 %collective-permute-done.22.refs_14_ = f32[1,128,128]{2,1,0:T(8,128)S(1)} collective-permute-done((f32[1,128,128]{2,1,0:T(8,128)S(1)}, f32[1,128,128]{2,1,0:T(8,128)S(1)}, u32[]{:S(2)}, u32[]{:S(2)}) %collective-permute-start.22) | collective-permute-done | bytes 65568 | tf_op jit(solution)/shard_map/ppermute | solution.py:16
  73.3 0.1 collective-permute-start.12
  73.4 2.7 %collective-permute-start.13 = (f32[4,128,128]{2,1,0:T(8,128)S(1)}, f32[4,128,128]{2,1,0:T(8,128)S(1)}, u32[]{:S(2)}, u32[]{:S(2)}) collective-permute-start(f32[4,128,128]{2,1,0:T(8,128)S(1)} %constant_dynamic-update-slice_fusion.3), channel_id=1, source_target_pairs={{0,24},{8,0},{16,8},{24,16},{1,25},{9,1},{17,9},{25,17},{2,26},{10... | collective-permute-start | bytes 786440 | tf_op jit(solution)/shard_map/ppermute | solution.py:16
  76.1 3.2 %collective-permute-start.34 = (f32[4,128,128]{2,1,0:T(8,128)S(1)}, f32[4,128,128]{2,1,0:T(8,128)S(1)}, u32[]{:S(2)}, u32[]{:S(2)}) collective-permute-start(f32[4,128,128]{2,1,0:T(8,128)S(1)} %bitcast.48), channel_id=1, source_target_pairs={{0,2},{1,3},{2,0},{3,1},{4,6},{5,7},{6,4},{7,5},{8,10},{9,11},{10,... | collective-permute-start | bytes 786440 | tf_op jit(solution)/shard_map/ppermute | solution.py:16
  79.2 2.3 %collective-permute-start.35 = (f32[4,128,128]{2,1,0:T(8,128)S(1)}, f32[4,128,128]{2,1,0:T(8,128)S(1)}, u32[]{:S(2)}, u32[]{:S(2)}) collective-permute-start(f32[4,128,128]{2,1,0:T(8,128)S(1)} %bitcast.49), channel_id=1, source_target_pairs={{0,3},{1,0},{2,1},{3,2},{4,7},{5,4},{6,5},{7,6},{8,11},{9,8},{10,9... | collective-permute-start | bytes 786440 | tf_op jit(solution)/shard_map/ppermute | solution.py:16
  81.6 0.1 collective-permute-start.24
  81.7 2.7 %collective-permute-start.25 = (f32[6,128,128]{2,1,0:T(8,128)S(1)}, f32[6,128,128]{2,1,0:T(8,128)S(1)}, u32[]{:S(2)}, u32[]{:S(2)}) collective-permute-start(f32[6,128,128]{2,1,0:T(8,128)S(1)} %constant_dynamic-update-slice_fusion.5), channel_id=1, source_target_pairs={{0,24},{8,0},{16,8},{24,16},{1,25},{9,1},{17,9},{25,17},{2,26},{10... | collective-permute-start | bytes 1179656 | tf_op jit(solution)/shard_map/ppermute | solution.py:16
  84.4 0.1 pad_add_fusion.pos_ref
  84.5 0.1 collective-permute-start.27
  84.6 6.2 %collective-permute-done.35.c3 = f32[4,128,128]{2,1,0:T(8,128)S(1)} collective-permute-done((f32[4,128,128]{2,1,0:T(8,128)S(1)}, f32[4,128,128]{2,1,0:T(8,128)S(1)}, u32[]{:S(2)}, u32[]{:S(2)}) %collective-permute-start.35) | collective-permute-done | bytes 262176 | tf_op jit(solution)/shard_map/ppermute | solution.py:16
  90.7 2.7 %collective-permute-start.28 = (f32[1,128,128]{2,1,0:T(8,128)S(1)}, f32[1,128,128]{2,1,0:T(8,128)S(1)}, u32[]{:S(2)}, u32[]{:S(2)}) collective-permute-start(f32[1,128,128]{2,1,0:T(8,128)S(1)} %slice.32), channel_id=1, source_target_pairs={{0,224},{32,0},{64,32},{96,64},{128,96},{160,128},{192,160},{224,1... | collective-permute-start | bytes 196616 | tf_op jit(solution)/shard_map/ppermute | solution.py:16
  93.4 5.3 %factor.1 = (bf16[256,1024]{1,0:T(8,128)(2,1)S(1)}, bf16[256,1024]{1,0:T(8,128)(2,1)S(1)}, bf16[256,1024]{1,0:T(8,128)(2,1)S(1)}, bf16[256,1024]{1,0:T(8,128)(2,1)S(1)}) custom-call(s32[4]{0:T(128)S(1)} %pad_add_fusion.pos_ref, f32[2,512,512]{2,1,0:T(8,128)S(1)} %copy-done.1, f32[2,128,128]{2,1,0:T(8,128)S(1)} %bitcast.44, ...), custom_call_target="tpu_custom_call" | custom-call | flops 3221225472 | bytes 6291456 | tf_op jit(solution)/shard_map/factor/pallas_call | solution.py:107
  98.8 0.0 copy-start
  98.8 2.9 %product.1 = (f32[1024,128]{1,0:T(8,128)S(1)}, f32[1024,128]{1,0:T(8,128)S(1)}) custom-call(s32[4]{0:T(128)S(1)} %pad_add_fusion.pos_ref, f32[2,128,128]{2,1,0:T(8,128)S(1)} %collective-permute-done.refs_0_, f32[2,128,128]{2,1,0:T(8,128)S(1)} %collective-permute-done.1.refs_1_, f32[6,128,128]{2,1,0:T(8,128)S(1)} %collective-permute-done.4.refs_2_, ...), custom_call_target="tpu_custom_call" | custom-call | flops 1610612736 | bytes 7340032 | tf_op jit(solution)/shard_map/product/pallas_call | solution.py:157
  101.7 2.3 %collective-permute-start.36 = (f32[1024,128]{1,0:T(8,128)S(1)}, f32[1024,128]{1,0:T(8,128)S(1)}, u32[]{:S(2)}, u32[]{:S(2)}) collective-permute-start(f32[1024,128]{1,0:T(8,128)S(1)} %get-tuple-element.44), channel_id=1, source_target_pairs={{0,4},{4,0},{1,5},{5,1},{2,6},{6,2},{3,7},{7,3},{8,12},{12,8},{9,1... | collective-permute-start | bytes 1572872 | tf_op jit(solution)/shard_map/ppermute | solution.py:20
  104.0 1.5 %collective-permute-done.36 = f32[1024,128]{1,0:T(8,128)S(1)} collective-permute-done((f32[1024,128]{1,0:T(8,128)S(1)}, f32[1024,128]{1,0:T(8,128)S(1)}, u32[]{:S(2)}, u32[]{:S(2)}) %collective-permute-start.36) | collective-permute-done | bytes 524320 | tf_op jit(solution)/shard_map/ppermute | solution.py:20
  105.6 1.6 %finish.1 = f32[16,128,128]{2,1,0:T(8,128)} custom-call(s32[4]{0:T(128)S(1)} %pad_add_fusion.pos_ref, f32[16,128,128]{2,1,0:T(8,128)S(1)} %bitcast.36, f32[8,128,128]{2,1,0:T(8,128)S(1)} %bitcast.45, f32[8,128,128]{2,1,0:T(8,128)S(1)} %bitcast.46), custom_call_target="tpu_custom_call" | custom-call | flops 262144 | bytes 3145728 | tf_op jit(solution)/shard_map/finish/pallas_call | solution.py:176
  (42 shorter events, 0.3 us)
Async XLA Ops:
  1.9 13.7 %collective-permute-start.7 = (f32[128,128]{1,0:T(8,128)S(1)}, f32[128,128]{1,0:T(8,128)S(1)}, u32[]{:S(2)}, u32[]{:S(2)}) collective-permute-start(f32[128,128]{1,0:T(8,128)S(1)} %fusion), channel_id=1, source_target_pairs={{0,128},{1,129},{2,130},{3,131},{4,132},{5,133},{6,134},{7,135},{8... | collective-permute-start | bytes 196616 | tf_op jit(solution)/shard_map/ppermute | solution.py:208
  11.5 9.5 %collective-permute-start = (f32[2,128,128]{2,1,0:T(8,128)S(1)}, f32[2,128,128]{2,1,0:T(8,128)S(1)}, u32[]{:S(2)}, u32[]{:S(2)}) collective-permute-start(f32[2,128,128]{2,1,0:T(8,128)S(1)} %bitcast.38), channel_id=1, source_target_pairs={{0,0},{4,1},{8,2},{12,3},{16,4},{20,5},{24,6},{28,7},{2,8},{6,9},{... | collective-permute-start | bytes 393224 | tf_op jit(solution)/shard_map/ppermute | solution.py:30
  21.1 11.8 %collective-permute-start.8 = (f32[128,128]{1,0:T(8,128)S(1)}, f32[128,128]{1,0:T(8,128)S(1)}, u32[]{:S(2)}, u32[]{:S(2)}) collective-permute-start(f32[128,128]{1,0:T(8,128)S(1)} %broadcast_select_fusion.1), channel_id=1, source_target_pairs={{0,64},{128,192},{1,65},{129,193},{2,66},{130,194},{3,67},{131,195... | collective-permute-start | bytes 196616 | tf_op jit(solution)/shard_map/ppermute | solution.py:208
  22.4 18.2 %collective-permute-start.1 = (f32[2,128,128]{2,1,0:T(8,128)S(1)}, f32[2,128,128]{2,1,0:T(8,128)S(1)}, u32[]{:S(2)}, u32[]{:S(2)}) collective-permute-start(f32[2,128,128]{2,1,0:T(8,128)S(1)} %bitcast.39), channel_id=1, source_target_pairs={{1,0},{5,1},{9,2},{13,3},{17,4},{21,5},{25,6},{29,7},{3,8},{7,9},{... | collective-permute-start | bytes 393224 | tf_op jit(solution)/shard_map/ppermute | solution.py:30
  26.4 22.3 %collective-permute-start.29 = (f32[2,128,128]{2,1,0:T(8,128)S(1)}, f32[2,128,128]{2,1,0:T(8,128)S(1)}, u32[]{:S(2)}, u32[]{:S(2)}) collective-permute-start(f32[2,128,128]{2,1,0:T(8,128)S(1)} %bitcast.40), channel_id=1, source_target_pairs={{0,1},{1,2},{2,3},{3,0},{4,5},{5,6},{6,7},{7,4},{8,9},{9,10},{10,1... | collective-permute-start | bytes 393224 | tf_op jit(solution)/shard_map/ppermute | solution.py:16
  26.4 24.5 %collective-permute-start.30 = (f32[2,128,128]{2,1,0:T(8,128)S(1)}, f32[2,128,128]{2,1,0:T(8,128)S(1)}, u32[]{:S(2)}, u32[]{:S(2)}) collective-permute-start(f32[2,128,128]{2,1,0:T(8,128)S(1)} %bitcast.41), channel_id=1, source_target_pairs={{0,2},{1,3},{2,0},{3,1},{4,6},{5,7},{6,4},{7,5},{8,10},{9,11},{10,... | collective-permute-start | bytes 393224 | tf_op jit(solution)/shard_map/ppermute | solution.py:16
  32.9 9.9 %collective-permute-start.2 = (f32[2,128,128]{2,1,0:T(8,128)S(1)}, f32[2,128,128]{2,1,0:T(8,128)S(1)}, u32[]{:S(2)}, u32[]{:S(2)}) collective-permute-start(f32[2,128,128]{2,1,0:T(8,128)S(1)} %collective-permute-done.refs_0_), channel_id=1, source_target_pairs={{0,32},{32,64},{64,96},{96,128},{128,160},{160,192},{192,224},{224... | collective-permute-start | bytes 393224 | tf_op jit(solution)/shard_map/ppermute | solution.py:16
  32.9 3.6 %collective-permute-start.14 = (f32[128,128]{1,0:T(8,128)S(1)}, f32[128,128]{1,0:T(8,128)S(1)}, u32[]{:S(2)}, u32[]{:S(2)}) collective-permute-start(f32[128,128]{1,0:T(8,128)S(1)} %broadcast_select_fusion.2), channel_id=1, source_target_pairs={{0,32},{64,96},{128,160},{192,224},{1,33},{65,97},{129,161},{193,2... | collective-permute-start | bytes 196616 | tf_op jit(solution)/shard_map/ppermute | solution.py:208
  36.4 6.3 %collective-permute-start.3 = (f32[2,128,128]{2,1,0:T(8,128)S(1)}, f32[2,128,128]{2,1,0:T(8,128)S(1)}, u32[]{:S(2)}, u32[]{:S(2)}) collective-permute-start(f32[2,128,128]{2,1,0:T(8,128)S(1)} %collective-permute-done.refs_0_), channel_id=1, source_target_pairs={{0,224},{32,0},{64,32},{96,64},{128,96},{160,128},{192,160},{224,1... | collective-permute-start | bytes 393224 | tf_op jit(solution)/shard_map/ppermute | solution.py:16
  40.6 10.3 %collective-permute-start.31 = (f32[2,128,128]{2,1,0:T(8,128)S(1)}, f32[2,128,128]{2,1,0:T(8,128)S(1)}, u32[]{:S(2)}, u32[]{:S(2)}) collective-permute-start(f32[2,128,128]{2,1,0:T(8,128)S(1)} %bitcast.42), channel_id=1, source_target_pairs={{0,3},{1,0},{2,1},{3,2},{4,7},{5,4},{6,5},{7,6},{8,11},{9,8},{10,9... | collective-permute-start | bytes 393224 | tf_op jit(solution)/shard_map/ppermute | solution.py:16
  42.7 14.3 %collective-permute-start.6 = (f32[2,128,128]{2,1,0:T(8,128)S(1)}, f32[2,128,128]{2,1,0:T(8,128)S(1)}, u32[]{:S(2)}, u32[]{:S(2)}) collective-permute-start(f32[2,128,128]{2,1,0:T(8,128)S(1)} %collective-permute-done.1.refs_1_), channel_id=1, source_target_pairs={{0,224},{32,0},{64,32},{96,64},{128,96},{160,128},{192,160},{224,1... | collective-permute-start | bytes 393224 | tf_op jit(solution)/shard_map/ppermute | solution.py:16
  42.7 4.6 %collective-permute-start.20 = (f32[128,128]{1,0:T(8,128)S(1)}, f32[128,128]{1,0:T(8,128)S(1)}, u32[]{:S(2)}, u32[]{:S(2)}) collective-permute-start(f32[128,128]{1,0:T(8,128)S(1)} %broadcast_select_fusion), channel_id=1, source_target_pairs={{0,4},{4,0},{1,5},{5,1},{2,6},{6,2},{3,7},{7,3},{8,12},{12,8},{9,1... | collective-permute-start | bytes 196616 | tf_op jit(solution)/shard_map/ppermute | solution.py:20
  47.4 7.0 %collective-permute-start.11 = (f32[2,128,128]{2,1,0:T(8,128)S(1)}, f32[2,128,128]{2,1,0:T(8,128)S(1)}, u32[]{:S(2)}, u32[]{:S(2)}) collective-permute-start(f32[2,128,128]{2,1,0:T(8,128)S(1)} %collective-permute-done.2.refs_22_), channel_id=1, source_target_pairs={{0,32},{32,64},{64,96},{96,128},{128,160},{160,192},{192,224},{224... | collective-permute-start | bytes 393224 | tf_op jit(solution)/shard_map/ppermute | solution.py:16
  48.6 44.8 %copy-start.1 = (f32[2,512,512]{2,1,0:T(8,128)S(1)}, f32[2,512,512]{2,1,0:T(8,128)}, u32[]{:S(2)}) copy-start(f32[2,512,512]{2,1,0:T(8,128)} %l_ref.1) | copy-start | bytes 6291460
  48.7 5.7 %collective-permute-start.9 = (f32[2,128,128]{2,1,0:T(8,128)S(1)}, f32[2,128,128]{2,1,0:T(8,128)S(1)}, u32[]{:S(2)}, u32[]{:S(2)}) collective-permute-start(f32[2,128,128]{2,1,0:T(8,128)S(1)} %collective-permute-done.3.refs_4_), channel_id=1, source_target_pairs={{0,224},{32,0},{64,32},{96,64},{128,96},{160,128},{192,160},{224,1... | collective-permute-start | bytes 393224 | tf_op jit(solution)/shard_map/ppermute | solution.py:16
  50.9 7.3 %collective-permute-start.21 = (f32[2,128,128]{2,1,0:T(8,128)S(1)}, f32[2,128,128]{2,1,0:T(8,128)S(1)}, u32[]{:S(2)}, u32[]{:S(2)}) collective-permute-start(f32[2,128,128]{2,1,0:T(8,128)S(1)} %pad_maximum_fusion.2), channel_id=1, source_target_pairs={{0,8},{8,0},{16,24},{24,16},{1,9},{9,1},{17,25},{25,17},{2,10},{10... | collective-permute-start | bytes 393224 | tf_op jit(solution)/shard_map/ppermute | solution.py:223
  50.9 7.6 %collective-permute-start.16 = (f32[2,128,128]{2,1,0:T(8,128)S(1)}, f32[2,128,128]{2,1,0:T(8,128)S(1)}, u32[]{:S(2)}, u32[]{:S(2)}) collective-permute-start(f32[2,128,128]{2,1,0:T(8,128)S(1)} %collective-permute-done.1.refs_1_), channel_id=1, source_target_pairs={{0,32},{32,64},{64,96},{96,128},{128,160},{160,192},{192,224},{224... | collective-permute-start | bytes 393224 | tf_op jit(solution)/shard_map/ppermute | solution.py:16
  54.4 11.0 %collective-permute-start.4 = (f32[6,128,128]{2,1,0:T(8,128)S(1)}, f32[6,128,128]{2,1,0:T(8,128)S(1)}, u32[]{:S(2)}, u32[]{:S(2)}) collective-permute-start(f32[6,128,128]{2,1,0:T(8,128)S(1)} %constant_dynamic-update-slice_fusion), channel_id=1, source_target_pairs={{0,8},{8,16},{16,24},{24,0},{1,9},{9,17},{17,25},{25,1},{2,10},{10... | collective-permute-start | bytes 1179656 | tf_op jit(solution)/shard_map/ppermute | solution.py:16
  54.4 14.1 %collective-permute-start.5 = (f32[6,128,128]{2,1,0:T(8,128)S(1)}, f32[6,128,128]{2,1,0:T(8,128)S(1)}, u32[]{:S(2)}, u32[]{:S(2)}) collective-permute-start(f32[6,128,128]{2,1,0:T(8,128)S(1)} %constant_dynamic-update-slice_fusion), channel_id=1, source_target_pairs={{0,24},{8,0},{16,8},{24,16},{1,25},{9,1},{17,9},{25,17},{2,26},{10... | collective-permute-start | bytes 1179656 | tf_op jit(solution)/shard_map/ppermute | solution.py:16
  57.0 4.1 %collective-permute-start.15 = (f32[2,128,128]{2,1,0:T(8,128)S(1)}, f32[2,128,128]{2,1,0:T(8,128)S(1)}, u32[]{:S(2)}, u32[]{:S(2)}) collective-permute-start(f32[2,128,128]{2,1,0:T(8,128)S(1)} %collective-permute-done.9.refs_6_), channel_id=1, source_target_pairs={{0,224},{32,0},{64,32},{96,64},{128,96},{160,128},{192,160},{224,1... | collective-permute-start | bytes 393224 | tf_op jit(solution)/shard_map/ppermute | solution.py:16
  58.2 5.3 %collective-permute-start.19 = (f32[2,128,128]{2,1,0:T(8,128)S(1)}, f32[2,128,128]{2,1,0:T(8,128)S(1)}, u32[]{:S(2)}, u32[]{:S(2)}) collective-permute-start(f32[2,128,128]{2,1,0:T(8,128)S(1)} %collective-permute-done.11.refs_20_), channel_id=1, source_target_pairs={{0,32},{32,64},{64,96},{96,128},{128,160},{160,192},{192,224},{224... | collective-permute-start | bytes 393224 | tf_op jit(solution)/shard_map/ppermute | solution.py:16
  58.5 9.9 %collective-permute-start.10 = (f32[2,128,128]{2,1,0:T(8,128)S(1)}, f32[2,128,128]{2,1,0:T(8,128)S(1)}, u32[]{:S(2)}, u32[]{:S(2)}) collective-permute-start(f32[2,128,128]{2,1,0:T(8,128)S(1)} %collective-permute-done.6.refs_5_), channel_id=1, source_target_pairs={{0,224},{32,0},{64,32},{96,64},{128,96},{160,128},{192,160},{224,1... | collective-permute-start | bytes 393224 | tf_op jit(solution)/shard_map/ppermute | solution.py:16
  61.1 10.0 %collective-permute-start.17 = (f32[2,128,128]{2,1,0:T(8,128)S(1)}, f32[2,128,128]{2,1,0:T(8,128)S(1)}, u32[]{:S(2)}, u32[]{:S(2)}) collective-permute-start(f32[2,128,128]{2,1,0:T(8,128)S(1)} %collective-permute-done.16.refs_23_), channel_id=1, source_target_pairs={{0,32},{32,64},{64,96},{96,128},{128,160},{160,192},{192,224},{224... | collective-permute-start | bytes 393224 | tf_op jit(solution)/shard_map/ppermute | solution.py:16
  63.5 9.9 %collective-permute-start.33 = (f32[4,128,128]{2,1,0:T(8,128)S(1)}, f32[4,128,128]{2,1,0:T(8,128)S(1)}, u32[]{:S(2)}, u32[]{:S(2)}) collective-permute-start(f32[4,128,128]{2,1,0:T(8,128)S(1)} %bitcast.47), channel_id=1, source_target_pairs={{0,1},{1,2},{2,3},{3,0},{4,5},{5,6},{6,7},{7,4},{8,9},{9,10},{10,1... | collective-permute-start | bytes 786440 | tf_op jit(solution)/shard_map/ppermute | solution.py:16
  65.3 28.1 %collective-permute-start.32 = (f32[4,2,128,128]{3,2,1,0:T(8,128)S(1)}, f32[4,2,128,128]{3,2,1,0:T(8,128)S(1)}, u32[]{:S(2)}, u32[]{:S(2)}) collective-permute-start(f32[4,2,128,128]{3,2,1,0:T(8,128)S(1)} %pad_maximum_fusion), channel_id=1, source_target_pairs={{0,4},{4,0},{1,5},{5,1},{2,6},{6,2},{3,7},{7,3},{8,12},{12,8},{9,1... | collective-permute-start | bytes 1572872 | tf_op jit(solution)/shard_map/ppermute | solution.py:20
  68.4 4.9 %collective-permute-start.22 = (f32[1,128,128]{2,1,0:T(8,128)S(1)}, f32[1,128,128]{2,1,0:T(8,128)S(1)}, u32[]{:S(2)}, u32[]{:S(2)}) collective-permute-start(f32[1,128,128]{2,1,0:T(8,128)S(1)} %slice.29), channel_id=1, source_target_pairs={{0,32},{32,64},{64,96},{96,128},{128,160},{160,192},{192,224},{224... | collective-permute-start | bytes 196616 | tf_op jit(solution)/shard_map/ppermute | solution.py:16
  68.4 4.9 %collective-permute-start.23 = (f32[1,128,128]{2,1,0:T(8,128)S(1)}, f32[1,128,128]{2,1,0:T(8,128)S(1)}, u32[]{:S(2)}, u32[]{:S(2)}) collective-permute-start(f32[1,128,128]{2,1,0:T(8,128)S(1)} %slice.30), channel_id=1, source_target_pairs={{0,224},{32,0},{64,32},{96,64},{128,96},{160,128},{192,160},{224,1... | collective-permute-start | bytes 196616 | tf_op jit(solution)/shard_map/ppermute | solution.py:16
  71.1 5.0 %collective-permute-start.18 = (f32[2,128,128]{2,1,0:T(8,128)S(1)}, f32[2,128,128]{2,1,0:T(8,128)S(1)}, u32[]{:S(2)}, u32[]{:S(2)}) collective-permute-start(f32[2,128,128]{2,1,0:T(8,128)S(1)} %collective-permute-done.10.refs_7_), channel_id=1, source_target_pairs={{0,224},{32,0},{64,32},{96,64},{128,96},{160,128},{192,160},{224,1... | collective-permute-start | bytes 393224 | tf_op jit(solution)/shard_map/ppermute | solution.py:16
  73.3 6.0 %collective-permute-start.26 = (f32[2,128,128]{2,1,0:T(8,128)S(1)}, f32[2,128,128]{2,1,0:T(8,128)S(1)}, u32[]{:S(2)}, u32[]{:S(2)}) collective-permute-start(f32[2,128,128]{2,1,0:T(8,128)S(1)} %collective-permute-done.17.refs_21_), channel_id=1, source_target_pairs={{0,32},{32,64},{64,96},{96,128},{128,160},{160,192},{192,224},{224... | collective-permute-start | bytes 393224 | tf_op jit(solution)/shard_map/ppermute | solution.py:16
  73.3 8.3 %collective-permute-start.12 = (f32[4,128,128]{2,1,0:T(8,128)S(1)}, f32[4,128,128]{2,1,0:T(8,128)S(1)}, u32[]{:S(2)}, u32[]{:S(2)}) collective-permute-start(f32[4,128,128]{2,1,0:T(8,128)S(1)} %constant_dynamic-update-slice_fusion.3), channel_id=1, source_target_pairs={{0,8},{8,16},{16,24},{24,0},{1,9},{9,17},{17,25},{25,1},{2,10},{10... | collective-permute-start | bytes 786440 | tf_op jit(solution)/shard_map/ppermute | solution.py:16
  73.4 8.3 %collective-permute-start.13 = (f32[4,128,128]{2,1,0:T(8,128)S(1)}, f32[4,128,128]{2,1,0:T(8,128)S(1)}, u32[]{:S(2)}, u32[]{:S(2)}) collective-permute-start(f32[4,128,128]{2,1,0:T(8,128)S(1)} %constant_dynamic-update-slice_fusion.3), channel_id=1, source_target_pairs={{0,24},{8,0},{16,8},{24,16},{1,25},{9,1},{17,9},{25,17},{2,26},{10... | collective-permute-start | bytes 786440 | tf_op jit(solution)/shard_map/ppermute | solution.py:16
  76.1 8.4 %collective-permute-start.34 = (f32[4,128,128]{2,1,0:T(8,128)S(1)}, f32[4,128,128]{2,1,0:T(8,128)S(1)}, u32[]{:S(2)}, u32[]{:S(2)}) collective-permute-start(f32[4,128,128]{2,1,0:T(8,128)S(1)} %bitcast.48), channel_id=1, source_target_pairs={{0,2},{1,3},{2,0},{3,1},{4,6},{5,7},{6,4},{7,5},{8,10},{9,11},{10,... | collective-permute-start | bytes 786440 | tf_op jit(solution)/shard_map/ppermute | solution.py:16
  79.2 11.5 %collective-permute-start.35 = (f32[4,128,128]{2,1,0:T(8,128)S(1)}, f32[4,128,128]{2,1,0:T(8,128)S(1)}, u32[]{:S(2)}, u32[]{:S(2)}) collective-permute-start(f32[4,128,128]{2,1,0:T(8,128)S(1)} %bitcast.49), channel_id=1, source_target_pairs={{0,3},{1,0},{2,1},{3,2},{4,7},{5,4},{6,5},{7,6},{8,11},{9,8},{10,9... | collective-permute-start | bytes 786440 | tf_op jit(solution)/shard_map/ppermute | solution.py:16
  81.6 17.1 %collective-permute-start.24 = (f32[6,128,128]{2,1,0:T(8,128)S(1)}, f32[6,128,128]{2,1,0:T(8,128)S(1)}, u32[]{:S(2)}, u32[]{:S(2)}) collective-permute-start(f32[6,128,128]{2,1,0:T(8,128)S(1)} %constant_dynamic-update-slice_fusion.5), channel_id=1, source_target_pairs={{0,8},{8,16},{16,24},{24,0},{1,9},{9,17},{17,25},{25,1},{2,10},{10... | collective-permute-start | bytes 1179656 | tf_op jit(solution)/shard_map/ppermute | solution.py:16
  81.7 17.0 %collective-permute-start.25 = (f32[6,128,128]{2,1,0:T(8,128)S(1)}, f32[6,128,128]{2,1,0:T(8,128)S(1)}, u32[]{:S(2)}, u32[]{:S(2)}) collective-permute-start(f32[6,128,128]{2,1,0:T(8,128)S(1)} %constant_dynamic-update-slice_fusion.5), channel_id=1, source_target_pairs={{0,24},{8,0},{16,8},{24,16},{1,25},{9,1},{17,9},{25,17},{2,26},{10... | collective-permute-start | bytes 1179656 | tf_op jit(solution)/shard_map/ppermute | solution.py:16
  84.5 14.3 %collective-permute-start.27 = (f32[1,128,128]{2,1,0:T(8,128)S(1)}, f32[1,128,128]{2,1,0:T(8,128)S(1)}, u32[]{:S(2)}, u32[]{:S(2)}) collective-permute-start(f32[1,128,128]{2,1,0:T(8,128)S(1)} %slice.31), channel_id=1, source_target_pairs={{0,32},{32,64},{64,96},{96,128},{128,160},{160,192},{192,224},{224... | collective-permute-start | bytes 196616 | tf_op jit(solution)/shard_map/ppermute | solution.py:16
  90.7 8.0 %collective-permute-start.28 = (f32[1,128,128]{2,1,0:T(8,128)S(1)}, f32[1,128,128]{2,1,0:T(8,128)S(1)}, u32[]{:S(2)}, u32[]{:S(2)}) collective-permute-start(f32[1,128,128]{2,1,0:T(8,128)S(1)} %slice.32), channel_id=1, source_target_pairs={{0,224},{32,0},{64,32},{96,64},{128,96},{160,128},{192,160},{224,1... | collective-permute-start | bytes 196616 | tf_op jit(solution)/shard_map/ppermute | solution.py:16
  98.8 6.8 %copy-start = (f32[16,128,1,128]{3,2,1,0:T(1,128)S(1)}, f32[16,128,1,128]{3,2,1,0:T(1,128)}, u32[]{:S(2)}) copy-start(f32[16,128,1,128]{3,2,1,0:T(1,128)} %param.2) | copy-start | bytes 3145732
  101.7 3.8 %collective-permute-start.36 = (f32[1024,128]{1,0:T(8,128)S(1)}, f32[1024,128]{1,0:T(8,128)S(1)}, u32[]{:S(2)}, u32[]{:S(2)}) collective-permute-start(f32[1024,128]{1,0:T(8,128)S(1)} %get-tuple-element.44), channel_id=1, source_target_pairs={{0,4},{4,0},{1,5},{5,1},{2,6},{6,2},{3,7},{7,3},{8,12},{12,8},{9,1... | collective-permute-start | bytes 1572872 | tf_op jit(solution)/shard_map/ppermute | solution.py:20
where the time goes:
time: 107 us
  starting transfers between devices  68.8 us (64%)
  waiting for transfers between devices  26 us (24%)
  Pallas kernels  9.92 us (9%)
  local copies, waits for them, and re-layouts  1.12 us (1%)
    ppermute x28, starting transfers between devices, shift(): return lax.ppermute(v, axis, [(i, (i + step) % size) for i in range(size)])  39.4 us
    ppermute x28, waiting for transfers between devices, shift(): return lax.ppermute(v, axis, [(i, (i + step) % size) for i in range(size)])  15.9 us
    ppermute x3, starting transfers between devices, spread(): got = lax.ppermute(v, 'z', [(i, i + reach) for i in range(0, Z, 2 * reach)])  12.2 us
    ppermute x3, starting transfers between devices, other_core(): return lax.ppermute(v, 'k', [(0, 1), (1, 0)])  9.06 us
    ppermute x2, starting transfers between devices, swap(): return lax.ppermute(v, ('x', 'k', 'y'), perm)  8.09 us
    ppermute x2, waiting for transfers between devices, swap(): return lax.ppermute(v, ('x', 'k', 'y'), perm)  5.45 us
    pallas_call x1, Pallas kernels, factor(): pl.pallas_call(body, out_shape=(half,) * 4, in_specs=[SMEM] + [VMEM] * 10...  5.33 us
    pallas_call x1, Pallas kernels, product(): pl.pallas_call(body, out_shape=(half, half), in_specs=[SMEM] + [VMEM] * (...  2.94 us
  transfers between devices with their start and end apart: 37, of which 10 were waited for; matrix products, arithmetic and copies ran while one was open for 0% of the time, Pallas kernels for 5%

commit v1 on v0

v1 whole, which is shorter than its diff:
```python
import jax
import jax.numpy as jnp
from jax import lax
from jax.experimental import pallas as pl
from jax.experimental.pallas import tpu as pltpu
from jax.sharding import Mesh
from jax.sharding import PartitionSpec as P

Z, X, K, Y = 8, 4, 2, 4
B = 128
FIRST = (0, 2, 1, 3)
SECOND = (1, 3, 0, 2)


def shift(v, axis, size, step):
    return lax.ppermute(v, axis, [(i, (i + step) % size) for i in range(size)])


def other_core(v):
    return lax.ppermute(v, "k", [(0, 1), (1, 0)])


def swap(v, choice):
    perm = []
    for x in range(X):
        for k in range(K):
            for y in range(Y):
                source = ((2 * k + (y >> 1)) * K + (y & 1)) * Y + choice[x]
                perm.append((source, (x * K + k) * Y + y))
    return lax.ppermute(v, ("x", "k", "y"), perm)


def after(value, *done):
    return lax.optimization_barrier((value, *done))[0]


def gather_y(v):
    return [v] + [shift(v, "y", Y, s) for s in range(1, Y)]


def split(v):
    high = v.astype(jnp.bfloat16)
    return high, (v - high.astype(jnp.float32)).astype(jnp.bfloat16)


def mul(a, b, transposed):
    dims = (((1,), (1 if transposed else 0,)), ((), ()))
    f = lambda u, v: lax.dot_general(u, v, dims, preferred_element_type=jnp.float32)
    return f(a[0], b[0]) + (f(a[0], b[1]) + f(a[1], b[0]))


VMEM = pl.BlockSpec(memory_space=pltpu.VMEM)
SMEM = pl.BlockSpec(memory_space=pltpu.SMEM)


def at_block(i, n=1):
    return pl.ds(pl.multiple_of(i * B, B), n * B)


def pick(table, i):
    return jnp.where(i == 0, table[0], jnp.where(i == 1, table[1], jnp.where(i == 2, table[2], table[3])))


def params(mib):
    return pltpu.CompilerParams(vmem_limit_bytes=mib * 2**20)


def cost(products, mib):
    return pl.CostEstimate(flops=int(products * 6 * 512 * 512 * 256), bytes_accessed=mib * 2**20, transcendentals=0)


WIDE = jax.ShapeDtypeStruct((2 * B, 4 * B), jnp.float32)
WIDE16 = jax.ShapeDtypeStruct((2 * B, 4 * B), jnp.bfloat16)
SQUARE16 = jax.ShapeDtypeStruct((4 * B, 4 * B), jnp.bfloat16)
Z16 = jax.ShapeDtypeStruct((2 * B, 8 * B), jnp.bfloat16)


def first_panel(pos, inverse, mine, theirs):
    def body(pos_ref, l_ref, m0, m1, m2, m3, th, w_ref, vh, vl, x1, l0h, l0l, l1h, l1l, xc):
        y = pos_ref[3]
        for s, m in enumerate((m0, m1, m2, m3)):
            lanes = at_block(lax.rem(y + (Y - s), Y))
            xc[:B, lanes] = m[0]
            xc[B:, lanes] = th[s, 0]
            x1[:B, lanes] = m[1]
            x1[B:, lanes] = th[s, 1]
        l0 = l0h[...], l0l[...] = split(l_ref[0])
        l1h[...], l1l[...] = split(l_ref[1])
        w = mul(split(xc[...]), l0, True)
        w_ref[...] = w
        vh[...], vl[...] = split(mul(split(w), l0, False))

    return pl.pallas_call(
        body,
        out_shape=(WIDE, WIDE16, WIDE16, WIDE) + (SQUARE16,) * 4,
        in_specs=[SMEM] + [VMEM] * 6,
        out_specs=(VMEM,) * 8,
        scratch_shapes=[pltpu.VMEM((2 * B, 4 * B), jnp.float32)],
        compiler_params=params(24),
        cost_estimate=cost(2, 7),
        name="first_panel",
    )(pos, inverse, *mine, theirs)


def second_panel(pos, panel, corner):
    def body(pos_ref, w_ref, vh, vl, x1, l0h, l0l, l1h, l1l, c0, c1, c2, c3, fh, fl, ah, al, gs, vg, bg, zz):
        z, x, k, y = (pos_ref[i] for i in range(4))
        for s, c in enumerate((c0, c1, c2, c3)):
            rows = at_block(lax.rem(y + (Y - s), Y))
            for i in range(4):
                table = (FIRST, SECOND)[i % 2]
                gs[rows, at_block(pick(table, x ^ 1 if i >= 2 else x))] = c[i]
        l0, l1, v, g = (l0h[...], l0l[...]), (l1h[...], l1l[...]), (vh[...], vl[...]), split(gs[...])

        @pl.when(k == 0)
        def _():
            vg[...] = mul(v, g, False)

        @pl.when(k == 1)
        def _():
            vg[...] = mul(v, g, True)

        row = lax.broadcasted_iota(jnp.int32, (2 * B, 4 * B), 0)
        col = lax.broadcasted_iota(jnp.int32, (2 * B, 4 * B), 1)
        block = 2 * (x & 1) + jnp.where(row < B, k, 1 - k)
        unit = jnp.where(col == block * B + (row & (B - 1)), 1.0, 0.0)
        corner_slab, low = z == 0, x < 2
        u = mul(split(x1[...] - vg[...]), l1, True)
        w = jnp.where(corner_slab, jnp.where(low, unit, 0.0), w_ref[...])
        u = jnp.where(corner_slab, jnp.where(low, 0.0, unit), u)
        zb = mul(split(u), l1, False)

        @pl.when(k == 0)
        def _():
            bg[...] = mul(split(zb), g, True)

        @pl.when(k == 1)
        def _():
            bg[...] = mul(split(zb), g, False)

        zt = mul(split(w - mul(split(bg[...]), l0, True)), l0, False)
        sign = jnp.where(corner_slab, -1.0, 1.0)
        zz[:, : 4 * B] = zt * sign
        zz[:, 4 * B :] = zb * sign
        beside = (x + jnp.where(k == 0, 3, 1)) & 3
        which = (pick(FIRST, x), pick(SECOND, x), pick(FIRST, beside), pick(SECOND, beside))
        for j in range(4):
            lanes = slice(j * B, (j + 1) * B)
            ah[:, lanes] = vh[:, at_block(which[j])]
            al[:, lanes] = vl[:, at_block(which[j])]
            for p in range(2):
                lanes = slice((4 * p + j) * B, (4 * p + j + 1) * B)
                fh[:, lanes], fl[:, lanes] = split(zz[:, at_block(4 * p + which[j])])

    return pl.pallas_call(
        body,
        out_shape=(Z16, Z16, WIDE16, WIDE16),
        in_specs=[SMEM] + [VMEM] * 12,
        out_specs=(VMEM,) * 4,
        scratch_shapes=[
            pltpu.VMEM((4 * B, 4 * B), jnp.float32),
            pltpu.VMEM((2 * B, 4 * B), jnp.float32),
            pltpu.VMEM((2 * B, 4 * B), jnp.float32),
            pltpu.VMEM((2 * B, 8 * B), jnp.float32),
        ],
        compiler_params=params(24),
        cost_estimate=cost(6, 6),
        name="second_panel",
    )(pos, *panel, *corner)


SLOTS = [(0, None)] + [(t, h) for t in (1, 2, 3) for h in (0, 1)] + [(4, None)]


def row_block(z, k, slot):
    t, h = SLOTS[slot]
    return 2 * lax.rem(z + jnp.where(k == 0, Z - t, t), Z) + (k if h is None else h)


def product(pos, pieces, zs):
    arrays, index = [], {}
    for i in range(8):
        for c in range(8):
            array, *at = pieces[i][c]
            for n, known in enumerate(arrays):
                if known is array:
                    break
            else:
                n = len(arrays)
                arrays.append(array)
            index[(i, c)] = (n, tuple(at))

    def body(pos_ref, *refs):
        xs = refs[: len(arrays)]
        zh, zl, ah, al, own, oth, xh, xl = refs[len(arrays) :]
        z, x, k = pos_ref[0], pos_ref[1], pos_ref[2]
        for (i, c), (n, at) in index.items():
            high, low = split(xs[n][at])
            xh[i * B : (i + 1) * B, c * B : (c + 1) * B] = high
            xl[i * B : (i + 1) * B, c * B : (c + 1) * B] = low
        res = mul((xh[...], xl[...]), (zh[...], zl[...]), True)
        own[...] = res[:, :B]
        oth[...] = res[:, B:]
        for i in range(8):
            block = row_block(z, k, i)
            rows = slice(i * B, (i + 1) * B)

            @pl.when((block == 0) & ((z != 0) | (x >= 2)))
            def _():
                own[rows, :] = jnp.zeros((B, B), jnp.float32)
                oth[rows, :] = jnp.zeros((B, B), jnp.float32)

            @pl.when((block == 1) & (z != 0))
            def _():
                part = mul((xh[rows, : 4 * B], xl[rows, : 4 * B]), (ah[...], al[...]), True)
                own[rows, :] = part[:, :B]
                oth[rows, :] = part[:, B:]

    half = jax.ShapeDtypeStruct((8 * B, B), jnp.float32)
    return pl.pallas_call(
        body,
        out_shape=(half, half),
        in_specs=[SMEM] + [VMEM] * (len(arrays) + 4),
        out_specs=(VMEM, VMEM),
        scratch_shapes=[pltpu.VMEM((8 * B, 8 * B), jnp.bfloat16)] * 2,
        compiler_params=params(32),
        cost_estimate=cost(8, 7),
        name="product",
    )(pos, *arrays, *zs)


def finish(pos, a, own, got):
    def body(pos_ref, a_ref, own_ref, got_ref, out_ref):
        z, k = pos_ref[0], pos_ref[2]
        for i in range(8):
            for core, ref in ((k, own_ref), (1 - k, got_ref)):
                block = row_block(z, core, i)
                out_ref[block] = jnp.where(z == 0, 0.0, a_ref[block]) - ref[i]

    return pl.pallas_call(
        body,
        out_shape=jax.ShapeDtypeStruct((2 * Z, B, B), jnp.float32),
        in_specs=[SMEM] + [VMEM] * 3,
        out_specs=VMEM,
        compiler_params=params(16),
        cost_estimate=cost(0, 3),
        name="finish",
    )(pos, a, own.reshape(Z, B, B), got.reshape(Z, B, B))


def shards(matrix, inverse_factors):
    z, x, k, y = (lax.axis_index(n) for n in ("z", "x", "k", "y"))
    pos = jnp.stack([z, x, k, y]).astype(jnp.int32)
    a = matrix.reshape(16, B, B)

    def around(v, axis, size):
        perm = [(2 * i, 2 * ((i + 1) % size)) for i in range(size)]
        perm += [(2 * i + 1, 2 * ((i - 1) % size) + 1) for i in range(size)]
        return lax.ppermute(v, (axis, "k"), perm)

    blocks = jnp.swapaxes(a[:2], 1, 2)
    fg = jnp.stack([swap(blocks, FIRST), swap(blocks, SECOND)])
    got = other_core(fg)
    slab = jnp.stack([jnp.where(k == 0, fg, got), jnp.where(k == 0, got, fg)])
    rows = gather_y(after(blocks, fg))

    corner = jnp.where(k == 0, fg[:, 1], fg[:, 0])

    def spread(v, reach):
        got = lax.ppermute(v, "z", [(i, i + reach) for i in range(0, Z, 2 * reach)])
        return jnp.where(z % (2 * reach) == reach, got, v)

    s0 = around(fg, "x", X)
    r1 = around(slab, "z", Z)
    corner = spread(after(corner, slab), 4)
    s1 = around(r1, "x", X)
    r2 = around(after(r1, s0, corner), "z", Z)
    corner = spread(corner, 2)
    theirs = other_core(jnp.stack(rows))
    s2 = around(after(r2, s1), "x", X)
    r3 = around(after(r2, s1, corner), "z", Z)
    panel = first_panel(pos, inverse_factors, rows, theirs)
    corner = spread(corner, 1)
    half = lax.dynamic_index_in_dim(after(r3, s2, corner), k, 0, keepdims=False)
    r4 = around(half, "z", Z)
    s3 = around(after(r3, s2), "x", X)
    got = lax.ppermute(corner, "x", [(0, 1), (1, 0), (2, 3), (3, 2)])
    corners = gather_y(jnp.concatenate([corner, got]))
    s4 = around(r4, "x", X)

    def piece(ring, side, *at):
        return [((ring, side)[j // 2], *at, j % 2, p) for p in range(2) for j in range(4)]

    pieces = [piece(fg, s0)]
    for ring, side in ((r1, s1), (r2, s2), (r3, s3)):
        pieces += [piece(ring, side, 0), piece(ring, side, 1)]
    pieces += [piece(r4, s4)]

    zs = second_panel(pos, panel, corners)
    own, other = product(pos, pieces, zs)
    return finish(pos, a, own, other_core(other)).reshape(16, B, 1, B)


def solution(mesh):
    fine = Mesh(mesh.devices.reshape(Z, X, K, Y), ("z", "x", "k", "y"))
    spec = P(None, "y", None, ("z", "x", "k"))
    return jax.shard_map(shards, mesh=fine, in_specs=(spec, P()), out_specs=spec, check_vma=False)
```

time: 107 us -> 95.6 us (0.89)
  starting transfers between devices: 68.8 us -> 53.4 us
  waiting for transfers between devices: 26 us -> 18.8 us
  other arithmetic: 1.06 us -> 5.05 us
  Pallas kernels: 9.92 us -> 13.2 us
  local copies, waits for them, and re-layouts: 1.12 us -> 4.18 us
    ppermute x28 -> x6, starting transfers between devices: 39.4 us -> 3.47 us  [shift(): return lax.ppermute(v, axis, [(i, (i + step) % size) for i in range(size)])]
    ppermute x0 -> x9, starting transfers between devices: none -> 21.9 us  [around(): return lax.ppermute(v, (axis, 'k'), perm)]
    ppermute x28 -> x6, waiting for transfers between devices: 15.9 us -> 4.9 us  [shift(): return lax.ppermute(v, axis, [(i, (i + step) % size) for i in range(size)])]
    ppermute x3, starting transfers between devices: 12.2 us -> 8.21 us  [spread(): got = lax.ppermute(v, 'z', [(i, i + reach) for i in range(0, Z, 2 * reach)])]
    ppermute x0 -> x9, waiting for transfers between devices: none -> 3.3 us  [around(): return lax.ppermute(v, (axis, 'k'), perm)]
    ppermute x3, starting transfers between devices: 9.06 us -> 12.1 us  [other_core(): return lax.ppermute(v, 'k', [(0, 1), (1, 0)])]
    pallas_call x1 -> x2, Pallas kernels: 5.33 us -> 7.66 us  [the longest x1 5.58 us: second_panel(): pl.pallas_call(body, out_shape=(Z16, Z16, WIDE16, WIDE16), in_specs=[SMEM...]
    squeeze x0 -> x1, local copies, waits for them, and re-layouts: none -> 1.66 us  [shards(): half = lax.dynamic_index_in_dim(after(r3, s2, corner), k, 0, keepdims=False)]
  transfers between devices with their start and end apart: 37 -> 24, of which waited for: 10 -> 9; matrix products, arithmetic and copies ran while one was open for 0% -> 6% of each run, Pallas kernels for 5% -> 8%
where the time goes in v1:
time: 95.6 us; the launch traced here: 94.8 us
  starting transfers between devices  53.4 us (56%)
  waiting for transfers between devices  18.8 us (20%)
  Pallas kernels  13.2 us (14%)
  other arithmetic  5.05 us (5%)
  local copies, waits for them, and re-layouts  4.18 us (4%)
    ppermute x9, starting transfers between devices, around(): return lax.ppermute(v, (axis, 'k'), perm)  21.9 us
    ppermute x3, starting transfers between devices, other_core(): return lax.ppermute(v, 'k', [(0, 1), (1, 0)])  12.1 us
    ppermute x3, starting transfers between devices, spread(): got = lax.ppermute(v, 'z', [(i, i + reach) for i in range(0, Z, 2 * reach)])  8.21 us
    ppermute x2, starting transfers between devices, swap(): return lax.ppermute(v, ('x', 'k', 'y'), perm)  7.15 us
    pallas_call x1, Pallas kernels, second_panel(): pl.pallas_call(body, out_shape=(Z16, Z16, WIDE16, WIDE16), in_specs=[SMEM...  5.58 us
    ppermute x2, waiting for transfers between devices, swap(): return lax.ppermute(v, ('x', 'k', 'y'), perm)  5.25 us
    ppermute x6, waiting for transfers between devices, shift(): return lax.ppermute(v, axis, [(i, (i + step) % size) for i in range(size)])  4.9 us
    pallas_call x1, Pallas kernels, product(): pl.pallas_call(body, out_shape=(half, half), in_specs=[SMEM] + [VMEM] * (...  3.84 us
  transfers between devices with their start and end apart: 24, of which 9 were waited for; matrix products, arithmetic and copies ran while one was open for 6% of the time, Pallas kernels for 8%

profile of v1, /device:TPU:1, one launch (start us, length us, event | category | flops | bytes accessed | tf_op | source)
XLA Modules:
  0.0 94.8 jit_solution(1357354408371833214)
XLA Ops:
  0.0 0.9 slice.12
  0.9 0.1 copy.5
  1.0 4.6 %collective-permute-start = (f32[2,128,128]{2,1,0:T(8,128)S(1)}, f32[2,128,128]{2,1,0:T(8,128)S(1)}, u32[]{:S(2)}, u32[]{:S(2)}) collective-permute-start(f32[2,128,128]{2,1,0:T(8,128)S(1)} %bitcast.28), channel_id=1, source_target_pairs={{0,0},{4,1},{8,2},{12,3},{16,4},{20,5},{24,6},{28,7},{2,8},{6,9},{... | collective-permute-start | bytes 393224 | tf_op jit(solution)/shard_map/ppermute | solution.py:30
  5.6 2.6 %collective-permute-start.1 = (f32[2,128,128]{2,1,0:T(8,128)S(1)}, f32[2,128,128]{2,1,0:T(8,128)S(1)}, u32[]{:S(2)}, u32[]{:S(2)}) collective-permute-start(f32[2,128,128]{2,1,0:T(8,128)S(1)} %bitcast.29), channel_id=1, source_target_pairs={{1,0},{5,1},{9,2},{13,3},{17,4},{21,5},{25,6},{29,7},{3,8},{7,9},{... | collective-permute-start | bytes 393224 | tf_op jit(solution)/shard_map/ppermute | solution.py:30
  8.2 2.7 %collective-permute-done = f32[2,128,128]{2,1,0:T(8,128)S(1)} collective-permute-done((f32[2,128,128]{2,1,0:T(8,128)S(1)}, f32[2,128,128]{2,1,0:T(8,128)S(1)}, u32[]{:S(2)}, u32[]{:S(2)}) %collective-permute-start) | collective-permute-done | bytes 131104 | tf_op jit(solution)/shard_map/ppermute | solution.py:30
  10.9 2.5 %collective-permute-done.1 = f32[2,128,128]{2,1,0:T(8,128)S(1)} collective-permute-done((f32[2,128,128]{2,1,0:T(8,128)S(1)}, f32[2,128,128]{2,1,0:T(8,128)S(1)}, u32[]{:S(2)}, u32[]{:S(2)}) %collective-permute-start.1) | collective-permute-done | bytes 131104 | tf_op jit(solution)/shard_map/ppermute | solution.py:30
  13.4 1.5 %collective-permute-start.3 = (f32[2,2,128,128]{3,2,1,0:T(8,128)S(1)}, f32[2,2,128,128]{3,2,1,0:T(8,128)S(1)}, u32[]{:S(2)}, u32[]{:S(2)}) collective-permute-start(f32[2,2,128,128]{3,2,1,0:T(8,128)S(1)} %pad_maximum_fusion.2.refs_0_), channel_id=1, source_target_pairs={{0,4},{4,0},{1,5},{5,1},{2,6},{6,2},{3,7},{7,3},{8,12},{12,8},{9,1... | collective-permute-start | bytes 786440 | tf_op jit(solution)/shard_map/ppermute | solution.py:20
  14.9 1.2 %collective-permute-done.3 = f32[2,2,128,128]{3,2,1,0:T(8,128)S(1)} collective-permute-done((f32[2,2,128,128]{3,2,1,0:T(8,128)S(1)}, f32[2,2,128,128]{3,2,1,0:T(8,128)S(1)}, u32[]{:S(2)}, u32[]{:S(2)}) %collective-permute-start.3) | collective-permute-done | bytes 262176 | tf_op jit(solution)/shard_map/ppermute | solution.py:20
  16.1 0.8 pad_maximum_fusion
  17.0 5.6 %collective-permute-start.4 = (f32[2,2,2,128,128]{4,3,2,1,0:T(8,128)}, f32[2,2,2,128,128]{4,3,2,1,0:T(8,128)S(1)}, u32[]{:S(2)}, u32[]{:S(2)}) collective-permute-start(f32[2,2,2,128,128]{4,3,2,1,0:T(8,128)} %pad_maximum_fusion), channel_id=1, source_target_pairs={{0,32},{32,64},{64,96},{96,128},{128,160},{160,192},{192,224},{224... | collective-permute-start | bytes 1572872 | tf_op jit(solution)/shard_map/ppermute | solution.py:259
  22.6 4.0 %collective-permute-start.6 = (f32[2,128,128]{2,1,0:T(8,128)S(1)}, f32[2,128,128]{2,1,0:T(8,128)}, u32[]{:S(2)}, u32[]{:S(2)}) collective-permute-start(f32[2,128,128]{2,1,0:T(8,128)S(1)} %fusion.2), channel_id=1, source_target_pairs={{0,128},{1,129},{2,130},{3,131},{4,132},{5,133},{6,134},{7,135},{8... | collective-permute-start | bytes 393224 | tf_op jit(solution)/shard_map/ppermute | solution.py:270
  26.6 5.8 %collective-permute-start.2 = (f32[2,2,128,128]{3,2,1,0:T(8,128)S(1)}, f32[2,2,128,128]{3,2,1,0:T(8,128)S(1)}, u32[]{:S(2)}, u32[]{:S(2)}) collective-permute-start(f32[2,2,128,128]{3,2,1,0:T(8,128)S(1)} %pad_maximum_fusion.2.refs_0_), channel_id=1, source_target_pairs={{0,8},{8,16},{16,24},{24,0},{4,28},{12,4},{20,12},{28,20},{1,9},{9... | collective-permute-start | bytes 786440 | tf_op jit(solution)/shard_map/ppermute | solution.py:259
  32.4 0.0 collective-permute-done.6
  32.4 3.3 %collective-permute-done.2.refs_1_ = f32[2,2,128,128]{3,2,1,0:T(8,128)S(1)} collective-permute-done((f32[2,2,128,128]{3,2,1,0:T(8,128)S(1)}, f32[2,2,128,128]{3,2,1,0:T(8,128)S(1)}, u32[]{:S(2)}, u32[]{:S(2)}) %collective-permute-start.2) | collective-permute-done | bytes 262176 | tf_op jit(solution)/shard_map/ppermute | solution.py:259
  35.7 0.7 copy-done.4
  36.4 0.0 collective-permute-done.4.refs_2_
  36.4 0.0 collective-permute-start.7
  36.4 3.1 %collective-permute-start.5 = (f32[2,2,2,128,128]{4,3,2,1,0:T(8,128)S(1)}, f32[2,2,2,128,128]{4,3,2,1,0:T(8,128)}, u32[]{:S(2)}, u32[]{:S(2)}) collective-permute-start(f32[2,2,2,128,128]{4,3,2,1,0:T(8,128)S(1)} %collective-permute-done.4.refs_2_), channel_id=1, source_target_pairs={{0,8},{8,16},{16,24},{24,0},{4,28},{12,4},{20,12},{28,20},{1,9},{9... | collective-permute-start | bytes 1572872 | tf_op jit(solution)/shard_map/ppermute | solution.py:259
  39.5 0.8 copy-done.2
  40.3 1.9 %collective-permute-start.9 = (f32[2,128,128]{2,1,0:T(8,128)S(1)}, f32[2,128,128]{2,1,0:T(8,128)}, u32[]{:S(2)}, u32[]{:S(2)}) collective-permute-start(f32[2,128,128]{2,1,0:T(8,128)S(1)} %broadcast_select_fusion.2), channel_id=1, source_target_pairs={{0,64},{128,192},{1,65},{129,193},{2,66},{130,194},{3,67},{131,195... | collective-permute-start | bytes 393224 | tf_op jit(solution)/shard_map/ppermute | solution.py:270
  42.3 0.0 collective-permute-start.15
  42.3 0.0 collective-permute-start.16
  42.3 2.7 %collective-permute-done.9 = f32[2,128,128]{2,1,0:T(8,128)} collective-permute-done((f32[2,128,128]{2,1,0:T(8,128)S(1)}, f32[2,128,128]{2,1,0:T(8,128)}, u32[]{:S(2)}, u32[]{:S(2)}) %collective-permute-start.9) | collective-permute-done | bytes 131104 | tf_op jit(solution)/shard_map/ppermute | solution.py:270
  45.0 0.1 collective-permute-start.17
  45.0 0.9 broadcast_select_fusion.1
  45.9 0.0 collective-permute-done.7.refs_4_
  46.0 0.0 collective-permute-done.5.refs_3_
  46.0 0.1 collective-permute-start.10
  46.1 3.1 %collective-permute-start.8 = (f32[2,2,2,128,128]{4,3,2,1,0:T(8,128)}, f32[2,2,2,128,128]{4,3,2,1,0:T(8,128)}, u32[]{:S(2)}, u32[]{:S(2)}) collective-permute-start(f32[2,2,2,128,128]{4,3,2,1,0:T(8,128)} %collective-permute-done.7.refs_4_), channel_id=1, source_target_pairs={{0,8},{8,16},{16,24},{24,0},{4,28},{12,4},{20,12},{28,20},{1,9},{9... | collective-permute-start | bytes 1572872 | tf_op jit(solution)/shard_map/ppermute | solution.py:259
  49.2 1.8 %collective-permute-done.15.m1 = f32[2,128,128]{2,1,0:T(8,128)S(1)} collective-permute-done((f32[2,128,128]{2,1,0:T(8,128)S(1)}, f32[2,128,128]{2,1,0:T(8,128)S(1)}, u32[]{:S(2)}, u32[]{:S(2)}) %collective-permute-start.15) | collective-permute-done | bytes 131104 | tf_op jit(solution)/shard_map/ppermute | solution.py:16
  51.0 2.2 %collective-permute-start.12 = (f32[2,128,128]{2,1,0:T(8,128)S(1)}, f32[2,128,128]{2,1,0:T(8,128)}, u32[]{:S(2)}, u32[]{:S(2)}) collective-permute-start(f32[2,128,128]{2,1,0:T(8,128)S(1)} %broadcast_select_fusion.1), channel_id=1, source_target_pairs={{0,32},{64,96},{128,160},{192,224},{1,33},{65,97},{129,161},{193,2... | collective-permute-start | bytes 393224 | tf_op jit(solution)/shard_map/ppermute | solution.py:270
  53.2 0.0 collective-permute-done.16.m2
  53.2 0.0 collective-permute-done.17.m3
  53.2 0.8 pad_maximum_fusion.1
  54.0 4.5 %collective-permute-start.18 = (f32[4,2,128,128]{3,2,1,0:T(8,128)}, f32[4,2,128,128]{3,2,1,0:T(8,128)S(1)}, u32[]{:S(2)}, u32[]{:S(2)}) collective-permute-start(f32[4,2,128,128]{3,2,1,0:T(8,128)} %pad_maximum_fusion.1), channel_id=1, source_target_pairs={{0,4},{4,0},{1,5},{5,1},{2,6},{6,2},{3,7},{7,3},{8,12},{12,8},{9,1... | collective-permute-start | bytes 1572872 | tf_op jit(solution)/shard_map/ppermute | solution.py:20
  58.5 0.0 collective-permute-done.12
  58.5 0.7 broadcast_select_fusion
  59.2 0.6 collective-permute-start.19
  59.8 0.0 collective-permute-done.10.refs_6_
  59.8 0.0 collective-permute-done.8.refs_5_
  59.8 1.7 %dynamic-slice_bitcast_fusion = f32[2,2,128,128]{3,2,1,0:T(8,128)} fusion(f32[2,2,2,128,128]{4,3,2,1,0:T(8,128)} %collective-permute-done.10.refs_6_, s32[]{:T(128)S(6)} %select_n.75), kind=kLoop, calls=%fused_computation.8 | loop fusion | bytes 524292 | tf_op jit(solution)/shard_map/jit(dynamic_index_in_dim)/squeeze | solution.py:284
  61.4 0.1 collective-permute-start.13
  61.5 2.3 %collective-permute-start.11 = (f32[2,2,2,128,128]{4,3,2,1,0:T(8,128)}, f32[2,2,2,128,128]{4,3,2,1,0:T(8,128)}, u32[]{:S(2)}, u32[]{:S(2)}) collective-permute-start(f32[2,2,2,128,128]{4,3,2,1,0:T(8,128)} %collective-permute-done.10.refs_6_), channel_id=1, source_target_pairs={{0,8},{8,16},{16,24},{24,0},{4,28},{12,4},{20,12},{28,20},{1,9},{9... | collective-permute-start | bytes 1572872 | tf_op jit(solution)/shard_map/ppermute | solution.py:259
  63.9 0.0 collective-permute-done.19
  63.9 1.6 %pad_maximum_fusion.3.c0 = f32[4,128,128]{2,1,0:T(8,128)} fusion(f32[2,128,128]{2,1,0:T(8,128)S(1)} %collective-permute-done.19, f32[2,128,128]{2,1,0:T(8,128)} %broadcast_select_fusion), kind=kLoop, calls=%fused_computation.7 | loop fusion | flops 65536 | bytes 524288 | tf_op jit(solution)/shard_map/concatenate | solution.py:288
  65.5 1.0 %collective-permute-start.20 = (f32[4,128,128]{2,1,0:T(8,128)}, f32[4,128,128]{2,1,0:T(8,128)}, u32[]{:S(2)}, u32[]{:S(2)}) collective-permute-start(f32[4,128,128]{2,1,0:T(8,128)} %pad_maximum_fusion.3.c0), channel_id=1, source_target_pairs={{0,1},{1,2},{2,3},{3,0},{4,5},{5,6},{6,7},{7,4},{8,9},{9,10},{10,1... | collective-permute-start | bytes 786440 | tf_op jit(solution)/shard_map/ppermute | solution.py:16
  66.5 0.1 collective-permute-start.21
  66.5 0.0 collective-permute-done.18.th
  66.6 2.3 %collective-permute-start.22 = (f32[4,128,128]{2,1,0:T(8,128)}, f32[4,128,128]{2,1,0:T(8,128)}, u32[]{:S(2)}, u32[]{:S(2)}) collective-permute-start(f32[4,128,128]{2,1,0:T(8,128)} %pad_maximum_fusion.3.c0), channel_id=1, source_target_pairs={{0,3},{1,0},{2,1},{3,2},{4,7},{5,4},{6,5},{7,6},{8,11},{9,8},{10,9... | collective-permute-start | bytes 786440 | tf_op jit(solution)/shard_map/ppermute | solution.py:16
  68.9 0.1 pad_add_fusion.pos_ref
  68.9 0.0 collective-permute-done.13.refs_8_
  68.9 1.8 %collective-permute-start.14 = (f32[2,2,128,128]{3,2,1,0:T(8,128)}, f32[2,2,128,128]{3,2,1,0:T(8,128)S(1)}, u32[]{:S(2)}, u32[]{:S(2)}) collective-permute-start(f32[2,2,128,128]{3,2,1,0:T(8,128)} %collective-permute-done.13.refs_8_), channel_id=1, source_target_pairs={{0,8},{8,16},{16,24},{24,0},{4,28},{12,4},{20,12},{28,20},{1,9},{9... | collective-permute-start | bytes 786440 | tf_op jit(solution)/shard_map/ppermute | solution.py:259
  70.8 2.1 %first_panel.1 = (f32[256,512]{1,0:T(8,128)S(1)}, bf16[256,512]{1,0:T(8,128)(2,1)S(1)}, bf16[256,512]{1,0:T(8,128)(2,1)S(1)}, f32[256,512]{1,0:T(8,128)S(1)}, bf...) custom-call(s32[4]{0:T(128)S(1)} %pad_add_fusion.pos_ref, ...), custom_call_target="tpu_custom_call" | custom-call | flops 805306368 | bytes 7340032 | tf_op jit(solution)/shard_map/first_panel/pallas_call | solution.py:93
  72.9 2.7 %collective-permute-done.20.c1 = f32[4,128,128]{2,1,0:T(8,128)} collective-permute-done((f32[4,128,128]{2,1,0:T(8,128)}, f32[4,128,128]{2,1,0:T(8,128)}, u32[]{:S(2)}, u32[]{:S(2)}) %collective-permute-start.20) | collective-permute-done | bytes 262176 | tf_op jit(solution)/shard_map/ppermute | solution.py:16
  75.6 0.0 collective-permute-done.21.c2
  75.6 0.4 collective-permute-done.22.c3
  76.0 5.6 %second_panel.1 = (bf16[256,1024]{1,0:T(8,128)(2,1)S(1)}, bf16[256,1024]{1,0:T(8,128)(2,1)S(1)}, bf16[256,512]{1,0:T(8,128)(2,1)S(1)}, bf16[256,512]{1,0:T(8,128)(2,1)S(1)}) custom-call(s32[4]{0:T(128)S(1)} %pad_add_fusion.pos_ref, f32[256,512]{1,0:T(8,128)S(1)} %get-tuple-element.33.w_ref, bf16[256,512]{1,0:T(8,128)(2,1)S(1)} %get-tuple-element.34.vh, ...), custom_call_target="tpu_custom_call" | custom-call | flops 2415919104 | bytes 6291456 | tf_op jit(solution)/shard_map/second_panel/pallas_call | solution.py:155
  81.6 0.0 collective-permute-done.14.refs_9_
  81.6 0.0 collective-permute-done.11.refs_7_
  81.6 0.0 copy-start.1
  81.6 3.8 %product.1 = (f32[1024,128]{1,0:T(8,128)S(1)}, f32[1024,128]{1,0:T(8,128)S(1)}) custom-call(s32[4]{0:T(128)S(1)} %pad_add_fusion.pos_ref, f32[2,2,128,128]{3,2,1,0:T(8,128)S(1)} %pad_maximum_fusion.2.refs_0_, f32[2,2,128,128]{3,2,1,0:T(8,128)S(1)} %copy-done.5, f32[2,2,2,128,128]{4,3,2,1,0:T(8,128)S(1)} %copy-done.3, ...), custom_call_target="tpu_custom_call" | custom-call | flops 3221225472 | bytes 7340032 | tf_op jit(solution)/shard_map/product/pallas_call | solution.py:220
  85.5 6.1 %collective-permute-start.23 = (f32[1024,128]{1,0:T(8,128)S(1)}, f32[1024,128]{1,0:T(8,128)S(1)}, u32[]{:S(2)}, u32[]{:S(2)}) collective-permute-start(f32[1024,128]{1,0:T(8,128)S(1)} %get-tuple-element.46), channel_id=1, source_target_pairs={{0,4},{4,0},{1,5},{5,1},{2,6},{6,2},{3,7},{7,3},{8,12},{12,8},{9,1... | collective-permute-start | bytes 1572872 | tf_op jit(solution)/shard_map/ppermute | solution.py:20
  91.6 1.5 %collective-permute-done.23 = f32[1024,128]{1,0:T(8,128)S(1)} collective-permute-done((f32[1024,128]{1,0:T(8,128)S(1)}, f32[1024,128]{1,0:T(8,128)S(1)}, u32[]{:S(2)}, u32[]{:S(2)}) %collective-permute-start.23) | collective-permute-done | bytes 524320 | tf_op jit(solution)/shard_map/ppermute | solution.py:20
  93.1 1.7 %finish.1 = f32[16,128,128]{2,1,0:T(8,128)} custom-call(s32[4]{0:T(128)S(1)} %pad_add_fusion.pos_ref, f32[16,128,128]{2,1,0:T(8,128)S(1)} %bitcast.27, f32[8,128,128]{2,1,0:T(8,128)S(1)} %bitcast.35, f32[8,128,128]{2,1,0:T(8,128)S(1)} %bitcast.36), custom_call_target="tpu_custom_call" | custom-call | bytes 3145728 | tf_op jit(solution)/shard_map/finish/pallas_call | solution.py:240
  (15 shorter events, 0.1 us)
Async XLA Ops:
  1.0 9.9 %collective-permute-start = (f32[2,128,128]{2,1,0:T(8,128)S(1)}, f32[2,128,128]{2,1,0:T(8,128)S(1)}, u32[]{:S(2)}, u32[]{:S(2)}) collective-permute-start(f32[2,128,128]{2,1,0:T(8,128)S(1)} %bitcast.28), channel_id=1, source_target_pairs={{0,0},{4,1},{8,2},{12,3},{16,4},{20,5},{24,6},{28,7},{2,8},{6,9},{... | collective-permute-start | bytes 393224 | tf_op jit(solution)/shard_map/ppermute | solution.py:30
  5.6 7.8 %collective-permute-start.1 = (f32[2,128,128]{2,1,0:T(8,128)S(1)}, f32[2,128,128]{2,1,0:T(8,128)S(1)}, u32[]{:S(2)}, u32[]{:S(2)}) collective-permute-start(f32[2,128,128]{2,1,0:T(8,128)S(1)} %bitcast.29), channel_id=1, source_target_pairs={{1,0},{5,1},{9,2},{13,3},{17,4},{21,5},{25,6},{29,7},{3,8},{7,9},{... | collective-permute-start | bytes 393224 | tf_op jit(solution)/shard_map/ppermute | solution.py:30
  13.4 2.7 %collective-permute-start.3 = (f32[2,2,128,128]{3,2,1,0:T(8,128)S(1)}, f32[2,2,128,128]{3,2,1,0:T(8,128)S(1)}, u32[]{:S(2)}, u32[]{:S(2)}) collective-permute-start(f32[2,2,128,128]{3,2,1,0:T(8,128)S(1)} %pad_maximum_fusion.2.refs_0_), channel_id=1, source_target_pairs={{0,4},{4,0},{1,5},{5,1},{2,6},{6,2},{3,7},{7,3},{8,12},{12,8},{9,1... | collective-permute-start | bytes 786440 | tf_op jit(solution)/shard_map/ppermute | solution.py:20
  17.0 53.8 %copy-start = (f32[2,512,512]{2,1,0:T(8,128)S(1)}, f32[2,512,512]{2,1,0:T(8,128)}, u32[]{:S(2)}) copy-start(f32[2,512,512]{2,1,0:T(8,128)} %l_ref.1) | copy-start | bytes 6291460
  17.0 19.4 %collective-permute-start.4 = (f32[2,2,2,128,128]{4,3,2,1,0:T(8,128)}, f32[2,2,2,128,128]{4,3,2,1,0:T(8,128)S(1)}, u32[]{:S(2)}, u32[]{:S(2)}) collective-permute-start(f32[2,2,2,128,128]{4,3,2,1,0:T(8,128)} %pad_maximum_fusion), channel_id=1, source_target_pairs={{0,32},{32,64},{64,96},{96,128},{128,160},{160,192},{192,224},{224... | collective-permute-start | bytes 1572872 | tf_op jit(solution)/shard_map/ppermute | solution.py:259
  22.6 9.8 %collective-permute-start.6 = (f32[2,128,128]{2,1,0:T(8,128)S(1)}, f32[2,128,128]{2,1,0:T(8,128)}, u32[]{:S(2)}, u32[]{:S(2)}) collective-permute-start(f32[2,128,128]{2,1,0:T(8,128)S(1)} %fusion.2), channel_id=1, source_target_pairs={{0,128},{1,129},{2,130},{3,131},{4,132},{5,133},{6,134},{7,135},{8... | collective-permute-start | bytes 393224 | tf_op jit(solution)/shard_map/ppermute | solution.py:270
  26.6 9.1 %collective-permute-start.2 = (f32[2,2,128,128]{3,2,1,0:T(8,128)S(1)}, f32[2,2,128,128]{3,2,1,0:T(8,128)S(1)}, u32[]{:S(2)}, u32[]{:S(2)}) collective-permute-start(f32[2,2,128,128]{3,2,1,0:T(8,128)S(1)} %pad_maximum_fusion.2.refs_0_), channel_id=1, source_target_pairs={{0,8},{8,16},{16,24},{24,0},{4,28},{12,4},{20,12},{28,20},{1,9},{9... | collective-permute-start | bytes 786440 | tf_op jit(solution)/shard_map/ppermute | solution.py:259
  32.4 9.9 %copy-start.6 = (f32[2,128,128]{2,1,0:T(8,128)}, f32[2,128,128]{2,1,0:T(8,128)S(1)}, u32[]{:S(2)}) copy-start(f32[2,128,128]{2,1,0:T(8,128)S(1)} %broadcast_select_fusion.2) | copy-start | bytes 393220
  35.7 0.7 copy-start.4
  36.4 9.5 %collective-permute-start.7 = (f32[2,2,2,128,128]{4,3,2,1,0:T(8,128)S(1)}, f32[2,2,2,128,128]{4,3,2,1,0:T(8,128)}, u32[]{:S(2)}, u32[]{:S(2)}) collective-permute-start(f32[2,2,2,128,128]{4,3,2,1,0:T(8,128)S(1)} %collective-permute-done.4.refs_2_), channel_id=1, source_target_pairs={{0,32},{32,64},{64,96},{96,128},{128,160},{160,192},{192,224},{224... | collective-permute-start | bytes 1572872 | tf_op jit(solution)/shard_map/ppermute | solution.py:259
  36.4 9.6 %collective-permute-start.5 = (f32[2,2,2,128,128]{4,3,2,1,0:T(8,128)S(1)}, f32[2,2,2,128,128]{4,3,2,1,0:T(8,128)}, u32[]{:S(2)}, u32[]{:S(2)}) collective-permute-start(f32[2,2,2,128,128]{4,3,2,1,0:T(8,128)S(1)} %collective-permute-done.4.refs_2_), channel_id=1, source_target_pairs={{0,8},{8,16},{16,24},{24,0},{4,28},{12,4},{20,12},{28,20},{1,9},{9... | collective-permute-start | bytes 1572872 | tf_op jit(solution)/shard_map/ppermute | solution.py:259
  39.5 0.8 copy-start.2
  40.3 4.7 %collective-permute-start.9 = (f32[2,128,128]{2,1,0:T(8,128)S(1)}, f32[2,128,128]{2,1,0:T(8,128)}, u32[]{:S(2)}, u32[]{:S(2)}) collective-permute-start(f32[2,128,128]{2,1,0:T(8,128)S(1)} %broadcast_select_fusion.2), channel_id=1, source_target_pairs={{0,64},{128,192},{1,65},{129,193},{2,66},{130,194},{3,67},{131,195... | collective-permute-start | bytes 393224 | tf_op jit(solution)/shard_map/ppermute | solution.py:270
  42.3 8.7 %collective-permute-start.15 = (f32[2,128,128]{2,1,0:T(8,128)S(1)}, f32[2,128,128]{2,1,0:T(8,128)S(1)}, u32[]{:S(2)}, u32[]{:S(2)}) collective-permute-start(f32[2,128,128]{2,1,0:T(8,128)S(1)} %bitcast.30), channel_id=1, source_target_pairs={{0,1},{1,2},{2,3},{3,0},{4,5},{5,6},{6,7},{7,4},{8,9},{9,10},{10,1... | collective-permute-start | bytes 393224 | tf_op jit(solution)/shard_map/ppermute | solution.py:16
  42.3 10.9 %collective-permute-start.16 = (f32[2,128,128]{2,1,0:T(8,128)S(1)}, f32[2,128,128]{2,1,0:T(8,128)S(1)}, u32[]{:S(2)}, u32[]{:S(2)}) collective-permute-start(f32[2,128,128]{2,1,0:T(8,128)S(1)} %bitcast.31), channel_id=1, source_target_pairs={{0,2},{1,3},{2,0},{3,1},{4,6},{5,7},{6,4},{7,5},{8,10},{9,11},{10,... | collective-permute-start | bytes 393224 | tf_op jit(solution)/shard_map/ppermute | solution.py:16
  45.0 8.2 %collective-permute-start.17 = (f32[2,128,128]{2,1,0:T(8,128)S(1)}, f32[2,128,128]{2,1,0:T(8,128)S(1)}, u32[]{:S(2)}, u32[]{:S(2)}) collective-permute-start(f32[2,128,128]{2,1,0:T(8,128)S(1)} %bitcast.32), channel_id=1, source_target_pairs={{0,3},{1,0},{2,1},{3,2},{4,7},{5,4},{6,5},{7,6},{8,11},{9,8},{10,9... | collective-permute-start | bytes 393224 | tf_op jit(solution)/shard_map/ppermute | solution.py:16
  46.0 13.8 %collective-permute-start.10 = (f32[2,2,2,128,128]{4,3,2,1,0:T(8,128)}, f32[2,2,2,128,128]{4,3,2,1,0:T(8,128)}, u32[]{:S(2)}, u32[]{:S(2)}) collective-permute-start(f32[2,2,2,128,128]{4,3,2,1,0:T(8,128)} %collective-permute-done.7.refs_4_), channel_id=1, source_target_pairs={{0,32},{32,64},{64,96},{96,128},{128,160},{160,192},{192,224},{224... | collective-permute-start | bytes 1572872 | tf_op jit(solution)/shard_map/ppermute | solution.py:259
  46.1 13.7 %collective-permute-start.8 = (f32[2,2,2,128,128]{4,3,2,1,0:T(8,128)}, f32[2,2,2,128,128]{4,3,2,1,0:T(8,128)}, u32[]{:S(2)}, u32[]{:S(2)}) collective-permute-start(f32[2,2,2,128,128]{4,3,2,1,0:T(8,128)} %collective-permute-done.7.refs_4_), channel_id=1, source_target_pairs={{0,8},{8,16},{16,24},{24,0},{4,28},{12,4},{20,12},{28,20},{1,9},{9... | collective-permute-start | bytes 1572872 | tf_op jit(solution)/shard_map/ppermute | solution.py:259
  51.0 7.6 %collective-permute-start.12 = (f32[2,128,128]{2,1,0:T(8,128)S(1)}, f32[2,128,128]{2,1,0:T(8,128)}, u32[]{:S(2)}, u32[]{:S(2)}) collective-permute-start(f32[2,128,128]{2,1,0:T(8,128)S(1)} %broadcast_select_fusion.1), channel_id=1, source_target_pairs={{0,32},{64,96},{128,160},{192,224},{1,33},{65,97},{129,161},{193,2... | collective-permute-start | bytes 393224 | tf_op jit(solution)/shard_map/ppermute | solution.py:270
  54.0 12.5 %collective-permute-start.18 = (f32[4,2,128,128]{3,2,1,0:T(8,128)}, f32[4,2,128,128]{3,2,1,0:T(8,128)S(1)}, u32[]{:S(2)}, u32[]{:S(2)}) collective-permute-start(f32[4,2,128,128]{3,2,1,0:T(8,128)} %pad_maximum_fusion.1), channel_id=1, source_target_pairs={{0,4},{4,0},{1,5},{5,1},{2,6},{6,2},{3,7},{7,3},{8,12},{12,8},{9,1... | collective-permute-start | bytes 1572872 | tf_op jit(solution)/shard_map/ppermute | solution.py:20
  59.2 4.6 %collective-permute-start.19 = (f32[2,128,128]{2,1,0:T(8,128)}, f32[2,128,128]{2,1,0:T(8,128)S(1)}, u32[]{:S(2)}, u32[]{:S(2)}) collective-permute-start(f32[2,128,128]{2,1,0:T(8,128)} %broadcast_select_fusion), channel_id=1, source_target_pairs={{0,8},{8,0},{16,24},{24,16},{1,9},{9,1},{17,25},{25,17},{2,10},{10... | collective-permute-start | bytes 393224 | tf_op jit(solution)/shard_map/ppermute | solution.py:287
  61.4 7.5 %collective-permute-start.13 = (f32[2,2,128,128]{3,2,1,0:T(8,128)}, f32[2,2,128,128]{3,2,1,0:T(8,128)}, u32[]{:S(2)}, u32[]{:S(2)}) collective-permute-start(f32[2,2,128,128]{3,2,1,0:T(8,128)} %dynamic-slice_bitcast_fusion), channel_id=1, source_target_pairs={{0,32},{32,64},{64,96},{96,128},{128,160},{160,192},{192,224},{224... | collective-permute-start | bytes 786440 | tf_op jit(solution)/shard_map/ppermute | solution.py:259
  61.5 20.1 %collective-permute-start.11 = (f32[2,2,2,128,128]{4,3,2,1,0:T(8,128)}, f32[2,2,2,128,128]{4,3,2,1,0:T(8,128)}, u32[]{:S(2)}, u32[]{:S(2)}) collective-permute-start(f32[2,2,2,128,128]{4,3,2,1,0:T(8,128)} %collective-permute-done.10.refs_6_), channel_id=1, source_target_pairs={{0,8},{8,16},{16,24},{24,0},{4,28},{12,4},{20,12},{28,20},{1,9},{9... | collective-permute-start | bytes 1572872 | tf_op jit(solution)/shard_map/ppermute | solution.py:259
  65.5 10.1 %collective-permute-start.20 = (f32[4,128,128]{2,1,0:T(8,128)}, f32[4,128,128]{2,1,0:T(8,128)}, u32[]{:S(2)}, u32[]{:S(2)}) collective-permute-start(f32[4,128,128]{2,1,0:T(8,128)} %pad_maximum_fusion.3.c0), channel_id=1, source_target_pairs={{0,1},{1,2},{2,3},{3,0},{4,5},{5,6},{6,7},{7,4},{8,9},{9,10},{10,1... | collective-permute-start | bytes 786440 | tf_op jit(solution)/shard_map/ppermute | solution.py:16
  66.5 9.2 %collective-permute-start.21 = (f32[4,128,128]{2,1,0:T(8,128)}, f32[4,128,128]{2,1,0:T(8,128)}, u32[]{:S(2)}, u32[]{:S(2)}) collective-permute-start(f32[4,128,128]{2,1,0:T(8,128)} %pad_maximum_fusion.3.c0), channel_id=1, source_target_pairs={{0,2},{1,3},{2,0},{3,1},{4,6},{5,7},{6,4},{7,5},{8,10},{9,11},{10,... | collective-permute-start | bytes 786440 | tf_op jit(solution)/shard_map/ppermute | solution.py:16
  66.6 9.4 %collective-permute-start.22 = (f32[4,128,128]{2,1,0:T(8,128)}, f32[4,128,128]{2,1,0:T(8,128)}, u32[]{:S(2)}, u32[]{:S(2)}) collective-permute-start(f32[4,128,128]{2,1,0:T(8,128)} %pad_maximum_fusion.3.c0), channel_id=1, source_target_pairs={{0,3},{1,0},{2,1},{3,2},{4,7},{5,4},{6,5},{7,6},{8,11},{9,8},{10,9... | collective-permute-start | bytes 786440 | tf_op jit(solution)/shard_map/ppermute | solution.py:16
  68.9 12.6 %collective-permute-start.14 = (f32[2,2,128,128]{3,2,1,0:T(8,128)}, f32[2,2,128,128]{3,2,1,0:T(8,128)S(1)}, u32[]{:S(2)}, u32[]{:S(2)}) collective-permute-start(f32[2,2,128,128]{3,2,1,0:T(8,128)} %collective-permute-done.13.refs_8_), channel_id=1, source_target_pairs={{0,8},{8,16},{16,24},{24,0},{4,28},{12,4},{20,12},{28,20},{1,9},{9... | collective-permute-start | bytes 786440 | tf_op jit(solution)/shard_map/ppermute | solution.py:259
  76.0 5.6 %copy-start.3 = (f32[2,2,2,128,128]{4,3,2,1,0:T(8,128)S(1)}, f32[2,2,2,128,128]{4,3,2,1,0:T(8,128)}, u32[]{:S(2)}) copy-start(f32[2,2,2,128,128]{4,3,2,1,0:T(8,128)} %copy-done.2) | copy-start | bytes 1572868
  76.0 5.6 %copy-start.5 = (f32[2,2,128,128]{3,2,1,0:T(8,128)S(1)}, f32[2,2,128,128]{3,2,1,0:T(8,128)}, u32[]{:S(2)}) copy-start(f32[2,2,128,128]{3,2,1,0:T(8,128)} %copy-done.4) | copy-start | bytes 786436
  81.6 11.5 %copy-start.1 = (f32[16,128,1,128]{3,2,1,0:T(1,128)S(1)}, f32[16,128,1,128]{3,2,1,0:T(1,128)}, u32[]{:S(2)}) copy-start(f32[16,128,1,128]{3,2,1,0:T(1,128)} %param.2) | copy-start | bytes 3145732
  85.5 7.6 %collective-permute-start.23 = (f32[1024,128]{1,0:T(8,128)S(1)}, f32[1024,128]{1,0:T(8,128)S(1)}, u32[]{:S(2)}, u32[]{:S(2)}) collective-permute-start(f32[1024,128]{1,0:T(8,128)S(1)} %get-tuple-element.46), channel_id=1, source_target_pairs={{0,4},{4,0},{1,5},{5,1},{2,6},{6,2},{3,7},{7,3},{8,12},{12,8},{9,1... | collective-permute-start | bytes 1572872 | tf_op jit(solution)/shard_map/ppermute | solution.py:20

commit v2 on v1

--- a/solution.py
+++ b/solution.py
@@ -69,54 +69,45 @@
     return pl.CostEstimate(flops=int(products * 6 * 512 * 512 * 256), bytes_accessed=mib * 2**20, transcendentals=0)
 
 
-WIDE = jax.ShapeDtypeStruct((2 * B, 4 * B), jnp.float32)
 WIDE16 = jax.ShapeDtypeStruct((2 * B, 4 * B), jnp.bfloat16)
-SQUARE16 = jax.ShapeDtypeStruct((4 * B, 4 * B), jnp.bfloat16)
 Z16 = jax.ShapeDtypeStruct((2 * B, 8 * B), jnp.bfloat16)
 
 
-def first_panel(pos, inverse, mine, theirs):
-    def body(pos_ref, l_ref, m0, m1, m2, m3, th, w_ref, vh, vl, x1, l0h, l0l, l1h, l1l, xc):
-        y = pos_ref[3]
-        for s, m in enumerate((m0, m1, m2, m3)):
-            lanes = at_block(lax.rem(y + (Y - s), Y))
-            xc[:B, lanes] = m[0]
-            xc[B:, lanes] = th[s, 0]
-            x1[:B, lanes] = m[1]
-            x1[B:, lanes] = th[s, 1]
-        l0 = l0h[...], l0l[...] = split(l_ref[0])
-        l1h[...], l1l[...] = split(l_ref[1])
-        w = mul(split(xc[...]), l0, True)
-        w_ref[...] = w
-        vh[...], vl[...] = split(mul(split(w), l0, False))
-
-    return pl.pallas_call(
-        body,
-        out_shape=(WIDE, WIDE16, WIDE16, WIDE) + (SQUARE16,) * 4,
-        in_specs=[SMEM] + [VMEM] * 6,
-        out_specs=(VMEM,) * 8,
-        scratch_shapes=[pltpu.VMEM((2 * B, 4 * B), jnp.float32)],
-        compiler_params=params(24),
-        cost_estimate=cost(2, 7),
-        name="first_panel",
-    )(pos, inverse, *mine, theirs)
-
-
-def second_panel(pos, panel, corner):
-    def body(pos_ref, w_ref, vh, vl, x1, l0h, l0l, l1h, l1l, c0, c1, c2, c3, fh, fl, ah, al, gs, vg, bg, zz):
+def factor(pos, inverse, gathered, got):
+    def body(pos_ref, l_ref, q0, q1, q2, q3, got_ref, fh, fl, ah, al, xc, gs, vg, bg, zz):
         z, x, k, y = (pos_ref[i] for i in range(4))
-        for s, c in enumerate((c0, c1, c2, c3)):
-            rows = at_block(lax.rem(y + (Y - s), Y))
-            for i in range(4):
-                table = (FIRST, SECOND)[i % 2]
-                gs[rows, at_block(pick(table, x ^ 1 if i >= 2 else x))] = c[i]
-        l0, l1, v, g = (l0h[...], l0l[...]), (l1h[...], l1l[...]), (vh[...], vl[...]), split(gs[...])
+        corner_slab, low = z == 0, x < 2
+
+        def place(rows, corner):
+            for s in range(Y):
+                from_y = lax.rem(y + (Y - s), Y)
+                for p in range(2):
+                    lanes = at_block(4 * p + from_y)
+                    xc[:B, lanes] = rows(s, 2 * k + p)
+                    xc[B:, lanes] = rows(s, 2 * (1 - k) + p)
+                for i in range(4):
+                    m = 2 * ((x + i // 2) & 1) + i % 2
+                    gs[at_block(m), at_block(from_y)] = corner(s, i)
+
+        mine = (q0, q1, q2, q3)
 
         @pl.when(k == 0)
         def _():
+            place(lambda s, i: mine[s][i], lambda s, i: got_ref[s, i])
+
+        @pl.when(k == 1)
+        def _():
+            place(lambda s, i: got_ref[s, i], lambda s, i: mine[s][i])
+
+        l0, l1, g = split(l_ref[0]), split(l_ref[1]), split(gs[...])
+        w = mul(split(xc[:, : 4 * B]), l0, True)
+        v = split(mul(split(w), l0, False))
+
+        @pl.when(low)
+        def _():
             vg[...] = mul(v, g, False)
 
-        @pl.when(k == 1)
+        @pl.when(x >= 2)
         def _():
             vg[...] = mul(v, g, True)
 
@@ -124,17 +115,16 @@
         col = lax.broadcasted_iota(jnp.int32, (2 * B, 4 * B), 1)
         block = 2 * (x & 1) + jnp.where(row < B, k, 1 - k)
         unit = jnp.where(col == block * B + (row & (B - 1)), 1.0, 0.0)
-        corner_slab, low = z == 0, x < 2
-        u = mul(split(x1[...] - vg[...]), l1, True)
-        w = jnp.where(corner_slab, jnp.where(low, unit, 0.0), w_ref[...])
+        u = mul(split(xc[:, 4 * B :] - vg[...]), l1, True)
+        w = jnp.where(corner_slab, jnp.where(low, unit, 0.0), w)
         u = jnp.where(corner_slab, jnp.where(low, 0.0, unit), u)
         zb = mul(split(u), l1, False)
 
-        @pl.when(k == 0)
+        @pl.when(low)
         def _():
             bg[...] = mul(split(zb), g, True)
 
-        @pl.when(k == 1)
+        @pl.when(x >= 2)
         def _():
             bg[...] = mul(split(zb), g, False)
 
@@ -142,39 +132,43 @@
         sign = jnp.where(corner_slab, -1.0, 1.0)
         zz[:, : 4 * B] = zt * sign
         zz[:, 4 * B :] = zb * sign
+        vg[...] = v[0].astype(jnp.float32)
+        bg[...] = v[1].astype(jnp.float32)
         beside = (x + jnp.where(k == 0, 3, 1)) & 3
         which = (pick(FIRST, x), pick(SECOND, x), pick(FIRST, beside), pick(SECOND, beside))
         for j in range(4):
             lanes = slice(j * B, (j + 1) * B)
-            ah[:, lanes] = vh[:, at_block(which[j])]
-            al[:, lanes] = vl[:, at_block(which[j])]
+            ah[:, lanes] = vg[:, at_block(which[j])].astype(jnp.bfloat16)
+            al[:, lanes] = bg[:, at_block(which[j])].astype(jnp.bfloat16)
             for p in range(2):
                 lanes = slice((4 * p + j) * B, (4 * p + j + 1) * B)
                 fh[:, lanes], fl[:, lanes] = split(zz[:, at_block(4 * p + which[j])])
 
+    wide = pltpu.VMEM((2 * B, 4 * B), jnp.float32)
     return pl.pallas_call(
         body,
         out_shape=(Z16, Z16, WIDE16, WIDE16),
-        in_specs=[SMEM] + [VMEM] * 12,
+        in_specs=[SMEM] + [VMEM] * 6,
         out_specs=(VMEM,) * 4,
         scratch_shapes=[
+            pltpu.VMEM((2 * B, 8 * B), jnp.float32),
             pltpu.VMEM((4 * B, 4 * B), jnp.float32),
-            pltpu.VMEM((2 * B, 4 * B), jnp.float32),
-            pltpu.VMEM((2 * B, 4 * B), jnp.float32),
+            wide,
+            wide,
             pltpu.VMEM((2 * B, 8 * B), jnp.float32),
         ],
-        compiler_params=params(24),
-        cost_estimate=cost(6, 6),
-        name="second_panel",
-    )(pos, *panel, *corner)
-
-
-SLOTS = [(0, None)] + [(t, h) for t in (1, 2, 3) for h in (0, 1)] + [(4, None)]
+        compiler_params=params(20),
+        cost_estimate=cost(8, 6),
+        name="factor",
+    )(pos, inverse, *gathered, got)
+
+
+SLOTS = [(0, 0)] + [(t, h) for t in (1, 2, 3) for h in (0, 1)] + [(4, 0)]
 
 
 def row_block(z, k, slot):
     t, h = SLOTS[slot]
-    return 2 * lax.rem(z + jnp.where(k == 0, Z - t, t), Z) + (k if h is None else h)
+    return 2 * lax.rem(z + jnp.where(k == 0, Z - t, t), Z) + (k if h == 0 else 1 - k)
 
 
 def product(pos, pieces, zs):
@@ -223,7 +217,7 @@
         in_specs=[SMEM] + [VMEM] * (len(arrays) + 4),
         out_specs=(VMEM, VMEM),
         scratch_shapes=[pltpu.VMEM((8 * B, 8 * B), jnp.bfloat16)] * 2,
-        compiler_params=params(32),
+        compiler_params=params(20),
         cost_estimate=cost(8, 7),
         name="product",
     )(pos, *arrays, *zs)
@@ -242,7 +236,7 @@
         out_shape=jax.ShapeDtypeStruct((2 * Z, B, B), jnp.float32),
         in_specs=[SMEM] + [VMEM] * 3,
         out_specs=VMEM,
-        compiler_params=params(16),
+        compiler_params=params(8),
         cost_estimate=cost(0, 3),
         name="finish",
     )(pos, a, own.reshape(Z, B, B), got.reshape(Z, B, B))
@@ -259,34 +253,33 @@
         return lax.ppermute(v, (axis, "k"), perm)
 
     blocks = jnp.swapaxes(a[:2], 1, 2)
-    fg = jnp.stack([swap(blocks, FIRST), swap(blocks, SECOND)])
-    got = other_core(fg)
-    slab = jnp.stack([jnp.where(k == 0, fg, got), jnp.where(k == 0, got, fg)])
-    rows = gather_y(after(blocks, fg))
-
-    corner = jnp.where(k == 0, fg[:, 1], fg[:, 0])
-
-    def spread(v, reach):
-        got = lax.ppermute(v, "z", [(i, i + reach) for i in range(0, Z, 2 * reach)])
-        return jnp.where(z % (2 * reach) == reach, got, v)
-
+    f0, g0 = swap(blocks, FIRST), swap(blocks, SECOND)
+
+    theirs = other_core(blocks)
+    columns = jnp.where(k == 0, jnp.concatenate([blocks, theirs]), jnp.concatenate([theirs, blocks]))
+    corner = jnp.where(x < 2, columns[1::2], columns[::2])
+
+    def to_core1(v, pairs):
+        return lax.ppermute(v, ("z", "k"), [(2 * i + c, 2 * j + 1) for i, c, j in pairs])
+
+    near, far = to_core1(corner, [(0, 0, 4), (0, 1, 2)]), to_core1(corner, [(0, 0, 6)])
+    fg = jnp.stack([f0, g0])
+    slab = jnp.stack([fg, other_core(fg)])
+    r1 = around(slab, "z", Z)
     s0 = around(fg, "x", X)
-    r1 = around(slab, "z", Z)
-    corner = spread(after(corner, slab), 4)
-    s1 = around(r1, "x", X)
-    r2 = around(after(r1, s0, corner), "z", Z)
-    corner = spread(corner, 2)
-    theirs = other_core(jnp.stack(rows))
-    s2 = around(after(r2, s1), "x", X)
-    r3 = around(after(r2, s1, corner), "z", Z)
-    panel = first_panel(pos, inverse_factors, rows, theirs)
-    corner = spread(corner, 1)
-    half = lax.dynamic_index_in_dim(after(r3, s2, corner), k, 0, keepdims=False)
-    r4 = around(half, "z", Z)
+    corner = jnp.where((z == 4) | (z == 2), near, jnp.where(z == 6, far, corner))
+    corner = jnp.where(z % 2 == 1, to_core1(corner, [(0, 0, 1), (2, 1, 3), (4, 1, 5), (6, 1, 7)]), corner)
+    beside = lax.ppermute(corner, ("x", "k"), [(2 * i + 1, 2 * (i ^ 1) + 1) for i in range(X)])
+    gathered = gather_y(jnp.where(k == 0, columns, jnp.concatenate([corner, beside])))
+
+    r2 = around(after(r1, s0), "z", Z)
+    s1 = around(after(r1, s0), "x", X)
+    r3 = around(after(r2, s1, gathered[0]), "z", Z)
+    s2 = around(after(r2, s1, gathered[0]), "x", X)
+    zs = factor(pos, inverse_factors, gathered, other_core(jnp.stack(gathered)))
+    r4 = around(after(r3[0], s2), "z", Z)
     s3 = around(after(r3, s2), "x", X)
-    got = lax.ppermute(corner, "x", [(0, 1), (1, 0), (2, 3), (3, 2)])
-    corners = gather_y(jnp.concatenate([corner, got]))
-    s4 = around(r4, "x", X)
+    s4 = around(after(r4, *zs), "x", X)
 
     def piece(ring, side, *at):
         return [((ring, side)[j // 2], *at, j % 2, p) for p in range(2) for j in range(4)]
@@ -296,7 +289,6 @@
         pieces += [piece(ring, side, 0), piece(ring, side, 1)]
     pieces += [piece(r4, s4)]
 
-    zs = second_panel(pos, panel, corners)
     own, other = product(pos, pieces, zs)
     return finish(pos, a, own, other_core(other)).reshape(16, B, 1, B)
 

time: 95.6 us -> 85.3 us (0.89)
  starting transfers between devices: 53.4 us -> 47.9 us
  other arithmetic: 5.05 us -> 1.33 us
  Pallas kernels: 13.2 us -> 11.4 us
  waiting for transfers between devices: 18.8 us -> 20 us
    ppermute x9, waiting for transfers between devices: 3.3 us -> 17.1 us  [around(): return lax.ppermute(v, (axis, 'k'), perm)]
    ppermute x2, waiting for transfers between devices: 5.25 us -> 0.13 us  [swap(): return lax.ppermute(v, ('x', 'k', 'y'), perm)]
    ppermute x6 -> x3, waiting for transfers between devices: 4.9 us -> 0.01 us  [shift(): return lax.ppermute(v, axis, [(i, (i + step) % size) for i in range(size)])]
    ppermute x3 -> x4, starting transfers between devices: 12.1 us -> 8.33 us  [other_core(): return lax.ppermute(v, 'k', [(0, 1), (1, 0)])]
    ppermute x4, starting transfers between devices: 8.76 us -> 12.1 us  [the longest x3 6.24 us: to_core1(): lax.ppermute(v, ('z', 'k'), [(2 * i + c, 2 * j + 1) for i, c, j in pairs])]
    ppermute x2, starting transfers between devices: 7.15 us -> 4.45 us  [swap(): return lax.ppermute(v, ('x', 'k', 'y'), perm)]
    ppermute x9, starting transfers between devices: 21.9 us -> 19.6 us  [around(): return lax.ppermute(v, (axis, 'k'), perm)]
    ppermute x4, waiting for transfers between devices: 2.67 us -> 0.43 us  [the longest x1 0.42 us: shards(): lax.ppermute(corner, ('x', 'k'), [(2 * i + 1, 2 * (i ^ 1) + 1) for i in r...]
  transfers between devices with their start and end apart: 24 -> 22, of which waited for: 9 -> 8; matrix products, arithmetic and copies ran while one was open for 6% -> 2% of each run, Pallas kernels for 8% -> 8%
where the time goes in v2:
time: 85.3 us; the launch traced here: 85.1 us
  starting transfers between devices  47.9 us (56%)
  waiting for transfers between devices  20 us (23%)
  Pallas kernels  11.4 us (13%)
  local copies, waits for them, and re-layouts  4.17 us (5%)
  other arithmetic  1.33 us (2%)
    ppermute x9, starting transfers between devices, around(): return lax.ppermute(v, (axis, 'k'), perm)  19.6 us
    ppermute x9, waiting for transfers between devices, around(): return lax.ppermute(v, (axis, 'k'), perm)  17.1 us
    ppermute x4, starting transfers between devices, other_core(): return lax.ppermute(v, 'k', [(0, 1), (1, 0)])  8.33 us
    pallas_call x1, Pallas kernels, factor(): pl.pallas_call(body, out_shape=(Z16, Z16, WIDE16, WIDE16), in_specs=[SMEM...  6.52 us
    ppermute x3, starting transfers between devices, to_core1(): lax.ppermute(v, ('z', 'k'), [(2 * i + c, 2 * j + 1) for i, c, j in pairs])  6.24 us
    ppermute x1, starting transfers between devices, shards(): lax.ppermute(corner, ('x', 'k'), [(2 * i + 1, 2 * (i ^ 1) + 1) for i in r...  5.91 us
    ppermute x2, starting transfers between devices, swap(): return lax.ppermute(v, ('x', 'k', 'y'), perm)  4.45 us
    ppermute x3, starting transfers between devices, shift(): return lax.ppermute(v, axis, [(i, (i + step) % size) for i in range(size)])  3.36 us
  transfers between devices with their start and end apart: 22, of which 8 were waited for; matrix products, arithmetic and copies ran while one was open for 2% of the time, Pallas kernels for 8%

profile of v2, /device:TPU:1, one launch (start us, length us, event | category | flops | bytes accessed | tf_op | source)
XLA Modules:
  0.0 85.1 jit_solution(13127663083733614141)
XLA Ops:
  0.0 0.9 %slice.15 = f32[2,128,1,128]{3,2,1,0:T(1,128)S(1)} slice(f32[16,128,1,128]{3,2,1,0:T(1,128)} %param.2), slice={[0:2], [0:128], [0:1], [0:128]} | slice | bytes 262144 | tf_op jit(solution)/shard_map/slice | solution.py:255
  0.9 0.1 copy.5
  1.0 3.3 %collective-permute-start.7 = (f32[2,128,128]{2,1,0:T(8,128)S(1)}, f32[2,128,128]{2,1,0:T(8,128)S(1)}, u32[]{:S(2)}, u32[]{:S(2)}) collective-permute-start(f32[2,128,128]{2,1,0:T(8,128)S(1)} %bitcast.34), channel_id=1, source_target_pairs={{0,4},{4,0},{1,5},{5,1},{2,6},{6,2},{3,7},{7,3},{8,12},{12,8},{9,1... | collective-permute-start | bytes 393224 | tf_op jit(solution)/shard_map/ppermute | solution.py:20
  4.3 1.9 %collective-permute-start = (f32[2,128,128]{2,1,0:T(8,128)S(1)}, f32[2,128,128]{2,1,0:T(8,128)S(1)}, u32[]{:S(2)}, u32[]{:S(2)}) collective-permute-start(f32[2,128,128]{2,1,0:T(8,128)S(1)} %bitcast.35), channel_id=1, source_target_pairs={{0,0},{4,1},{8,2},{12,3},{16,4},{20,5},{24,6},{28,7},{2,8},{6,9},{... | collective-permute-start | bytes 393224 | tf_op jit(solution)/shard_map/ppermute | solution.py:30
  6.3 2.5 %collective-permute-start.1 = (f32[2,128,128]{2,1,0:T(8,128)S(1)}, f32[2,128,128]{2,1,0:T(8,128)S(1)}, u32[]{:S(2)}, u32[]{:S(2)}) collective-permute-start(f32[2,128,128]{2,1,0:T(8,128)S(1)} %bitcast.36), channel_id=1, source_target_pairs={{1,0},{5,1},{9,2},{13,3},{17,4},{21,5},{25,6},{29,7},{3,8},{7,9},{... | collective-permute-start | bytes 393224 | tf_op jit(solution)/shard_map/ppermute | solution.py:30
  8.8 0.0 collective-permute-done.7
  8.9 4.9 %collective-permute-start.8 = (f32[2,128,128]{2,1,0:T(8,128)S(1)}, f32[2,128,128]{2,1,0:T(8,128)S(1)}, u32[]{:S(2)}, u32[]{:S(2)}) collective-permute-start(f32[2,128,128]{2,1,0:T(8,128)S(1)} %slice_select_fusion), channel_id=1, source_target_pairs={{0,132},{4,68},{1,133},{5,69},{2,134},{6,70},{3,135},{7,71},{8,140... | collective-permute-start | bytes 393224 | tf_op jit(solution)/shard_map/ppermute | solution.py:263
  13.8 0.7 collective-permute-start.9
  14.4 0.0 collective-permute-done
  14.5 0.1 collective-permute-done.1
  14.6 4.9 %collective-permute-start.3 = (f32[2,2,128,128]{3,2,1,0:T(8,128)S(1)}, f32[2,2,128,128]{3,2,1,0:T(8,128)S(1)}, u32[]{:S(2)}, u32[]{:S(2)}) collective-permute-start(f32[2,2,128,128]{3,2,1,0:T(8,128)S(1)} %get-tuple-element.28.refs_0_), channel_id=1, source_target_pairs={{0,4},{4,0},{1,5},{5,1},{2,6},{6,2},{3,7},{7,3},{8,12},{12,8},{9,1... | collective-permute-start | bytes 786440 | tf_op jit(solution)/shard_map/ppermute | solution.py:20
  19.5 0.0 collective-permute-done.8
  19.5 0.0 collective-permute-done.9
  19.6 0.7 collective-permute-start.10
  20.3 0.4 collective-permute-done.3
  20.7 1.4 %collective-permute-start.4 = (f32[2,2,2,128,128]{4,3,2,1,0:T(8,128)S(1)}, f32[2,2,2,128,128]{4,3,2,1,0:T(8,128)S(1)}, u32[]{:S(2)}, u32[]{:S(2)}) collective-permute-start(f32[2,2,2,128,128]{4,3,2,1,0:T(8,128)S(1)} %pad_maximum_fusion.1), channel_id=1, source_target_pairs={{0,32},{32,64},{64,96},{96,128},{128,160},{160,192},{192,224},{224... | collective-permute-start | bytes 1572872 | tf_op jit(solution)/shard_map/ppermute | solution.py:253
  22.1 0.0 collective-permute-done.10
  22.1 5.9 %collective-permute-start.11 = (f32[2,128,128]{2,1,0:T(8,128)S(1)}, f32[2,128,128]{2,1,0:T(8,128)S(1)}, u32[]{:S(2)}, u32[]{:S(2)}) collective-permute-start(f32[2,128,128]{2,1,0:T(8,128)S(1)} %broadcast_select_fusion), channel_id=1, source_target_pairs={{4,12},{12,4},{20,28},{28,20},{5,13},{13,5},{21,29},{29,21},{6,14}... | collective-permute-start | bytes 393224 | tf_op jit(solution)/shard_map/ppermute | solution.py:272
  28.1 2.5 %collective-permute-start.2 = (f32[2,2,128,128]{3,2,1,0:T(8,128)S(1)}, f32[2,2,128,128]{3,2,1,0:T(8,128)S(1)}, u32[]{:S(2)}, u32[]{:S(2)}) collective-permute-start(f32[2,2,128,128]{3,2,1,0:T(8,128)S(1)} %get-tuple-element.28.refs_0_), channel_id=1, source_target_pairs={{0,8},{8,16},{16,24},{24,0},{4,28},{12,4},{20,12},{28,20},{1,9},{9... | collective-permute-start | bytes 786440 | tf_op jit(solution)/shard_map/ppermute | solution.py:253
  30.6 0.4 collective-permute-done.11
  31.0 0.9 %collective-permute-start.16 = (f32[4,128,128]{2,1,0:T(8,128)S(1)}, f32[4,128,128]{2,1,0:T(8,128)S(1)}, u32[]{:S(2)}, u32[]{:S(2)}) collective-permute-start(f32[4,128,128]{2,1,0:T(8,128)S(1)} %maximum_select_fusion.1.q0), channel_id=1, source_target_pairs={{0,1},{1,2},{2,3},{3,0},{4,5},{5,6},{6,7},{7,4},{8,9},{9,10},{10,1... | collective-permute-start | bytes 786440 | tf_op jit(solution)/shard_map/ppermute | solution.py:16
  31.9 2.0 %collective-permute-start.17 = (f32[4,128,128]{2,1,0:T(8,128)S(1)}, f32[4,128,128]{2,1,0:T(8,128)S(1)}, u32[]{:S(2)}, u32[]{:S(2)}) collective-permute-start(f32[4,128,128]{2,1,0:T(8,128)S(1)} %maximum_select_fusion.1.q0), channel_id=1, source_target_pairs={{0,2},{1,3},{2,0},{3,1},{4,6},{5,7},{6,4},{7,5},{8,10},{9,11},{10,... | collective-permute-start | bytes 786440 | tf_op jit(solution)/shard_map/ppermute | solution.py:16
  33.9 0.5 collective-permute-start.18
  34.4 0.0 collective-permute-done.2.refs_1_
  34.4 0.0 copy-start.4
  34.4 0.7 copy-done.4
  35.1 0.0 collective-permute-done.4.refs_2_
  35.1 4.3 %collective-permute-start.5 = (f32[2,2,2,128,128]{4,3,2,1,0:T(8,128)S(1)}, f32[2,2,2,128,128]{4,3,2,1,0:T(8,128)S(1)}, u32[]{:S(2)}, u32[]{:S(2)}) collective-permute-start(f32[2,2,2,128,128]{4,3,2,1,0:T(8,128)S(1)} %collective-permute-done.4.refs_2_), channel_id=1, source_target_pairs={{0,8},{8,16},{16,24},{24,0},{4,28},{12,4},{20,12},{28,20},{1,9},{9... | collective-permute-start | bytes 1572872 | tf_op jit(solution)/shard_map/ppermute | solution.py:253
  39.5 5.6 %collective-permute-start.6 = (f32[2,2,2,128,128]{4,3,2,1,0:T(8,128)S(1)}, f32[2,2,2,128,128]{4,3,2,1,0:T(8,128)}, u32[]{:S(2)}, u32[]{:S(2)}) collective-permute-start(f32[2,2,2,128,128]{4,3,2,1,0:T(8,128)S(1)} %collective-permute-done.4.refs_2_), channel_id=1, source_target_pairs={{0,32},{32,64},{64,96},{96,128},{128,160},{160,192},{192,224},{224... | collective-permute-start | bytes 1572872 | tf_op jit(solution)/shard_map/ppermute | solution.py:253
  45.1 0.0 collective-permute-done.16.q1
  45.1 0.0 collective-permute-done.17.q2
  45.1 0.0 collective-permute-done.18.q3
  45.2 1.0 %pad_maximum_fusion = f32[4,4,128,128]{3,2,1,0:T(8,128)} fusion(f32[1,4,128,128]{3,2,1,0:T(8,128)S(1)} %bitcast.33, f32[1,4,128,128]{3,2,1,0:T(8,128)S(1)} %bitcast.32, f32[1,4,128,128]{3,2,1,0:T(8,128)S(1)} %bitcast.31, f32[1,4,128,128]{3,2,1,0:T(8,128)S(1)} %fusion), kind=kLoop, calls=%fused_computation | loop fusion | flops 786432 | bytes 2097152 | tf_op jit(solution)/shard_map/stack | solution.py:279
  46.2 0.0 collective-permute-start.19
  46.2 0.0 collective-permute-done.5.refs_3_
  46.2 0.0 copy-start.2
  46.2 0.8 copy-done.2
  47.0 4.2 %collective-permute-done.6.refs_4_ = f32[2,2,2,128,128]{4,3,2,1,0:T(8,128)} collective-permute-done((f32[2,2,2,128,128]{4,3,2,1,0:T(8,128)S(1)}, f32[2,2,2,128,128]{4,3,2,1,0:T(8,128)}, u32[]{:S(2)}, u32[]{:S(2)}) %collective-permute-start.6) | collective-permute-done | bytes 524320 | tf_op jit(solution)/shard_map/ppermute | solution.py:253
  51.2 3.2 %collective-permute-start.13 = (f32[2,2,2,128,128]{4,3,2,1,0:T(8,128)}, f32[2,2,2,128,128]{4,3,2,1,0:T(8,128)S(1)}, u32[]{:S(2)}, u32[]{:S(2)}) collective-permute-start(f32[2,2,2,128,128]{4,3,2,1,0:T(8,128)} %collective-permute-done.6.refs_4_), channel_id=1, source_target_pairs={{0,32},{32,64},{64,96},{96,128},{128,160},{160,192},{192,224},{224... | collective-permute-start | bytes 1572872 | tf_op jit(solution)/shard_map/ppermute | solution.py:253
  54.4 0.7 collective-permute-start.12
  55.2 0.1 pad_add_fusion.pos_ref
  55.2 5.6 %collective-permute-done.13.refs_6_ = f32[2,2,2,128,128]{4,3,2,1,0:T(8,128)S(1)} collective-permute-done((f32[2,2,2,128,128]{4,3,2,1,0:T(8,128)}, f32[2,2,2,128,128]{4,3,2,1,0:T(8,128)S(1)}, u32[]{:S(2)}, u32[]{:S(2)}) %collective-permute-start.13) | collective-permute-done | bytes 524320 | tf_op jit(solution)/shard_map/ppermute | solution.py:253
  60.9 0.0 copy-start.3
  60.9 2.1 %collective-permute-done.12.refs_5_ = f32[2,2,2,128,128]{4,3,2,1,0:T(8,128)} collective-permute-done((f32[2,2,2,128,128]{4,3,2,1,0:T(8,128)}, f32[2,2,2,128,128]{4,3,2,1,0:T(8,128)}, u32[]{:S(2)}, u32[]{:S(2)}) %collective-permute-start.12) | collective-permute-done | bytes 524320 | tf_op jit(solution)/shard_map/ppermute | solution.py:253
  63.0 1.0 %collective-permute-start.15 = (f32[2,2,128,128]{3,2,1,0:T(8,128)S(1)}, f32[2,2,128,128]{3,2,1,0:T(8,128)S(1)}, u32[]{:S(2)}, u32[]{:S(2)}) collective-permute-start(f32[2,2,128,128]{3,2,1,0:T(8,128)S(1)} %slice_bitcast_fusion), channel_id=1, source_target_pairs={{0,32},{32,64},{64,96},{96,128},{128,160},{160,192},{192,224},{224... | collective-permute-start | bytes 786440 | tf_op jit(solution)/shard_map/ppermute | solution.py:253
  64.0 0.7 collective-permute-start.14
  64.7 0.0 collective-permute-done.19.got_ref
  64.7 0.0 copy-start.1
  64.7 1.6 %copy-done.1 = f32[2,512,512]{2,1,0:T(8,128)S(1)} copy-done((f32[2,512,512]{2,1,0:T(8,128)S(1)}, f32[2,512,512]{2,1,0:T(8,128)}, u32[]{:S(2)}) %copy-start.1) | copy-done | bytes 2097176
  66.3 0.0 copy-start.5
  66.3 6.5 %factor.1 = (bf16[256,1024]{1,0:T(8,128)(2,1)S(1)}, bf16[256,1024]{1,0:T(8,128)(2,1)S(1)}, bf16[256,512]{1,0:T(8,128)(2,1)S(1)}, bf16[256,512]{1,0:T(8,128)(2,1)S(1)}) custom-call(s32[4]{0:T(128)S(1)} %pad_add_fusion.pos_ref, f32[2,512,512]{2,1,0:T(8,128)S(1)} %copy-done.1, f32[4,128,128]{2,1,0:T(8,128)S(1)} %maximum_select_fusion.1.q0, ...), custom_call_target="tpu_custom_call" | custom-call | flops 3221225472 | bytes 6291456 | tf_op jit(solution)/shard_map/factor/pallas_call | solution.py:148
  72.8 0.0 collective-permute-done.15.refs_8_
  72.9 0.0 copy-start
  72.9 0.1 collective-permute-start.20
  73.0 5.2 %collective-permute-done.20.refs_9_ = f32[2,2,128,128]{3,2,1,0:T(8,128)S(1)} collective-permute-done((f32[2,2,128,128]{3,2,1,0:T(8,128)S(1)}, f32[2,2,128,128]{3,2,1,0:T(8,128)S(1)}, u32[]{:S(2)}, u32[]{:S(2)}) %collective-permute-start.20) | collective-permute-done | bytes 262176 | tf_op jit(solution)/shard_map/ppermute | solution.py:253
  78.2 0.0 collective-permute-done.14.refs_7_
  78.2 0.0 copy-done.3
  78.2 0.0 copy-done.5
  78.2 3.2 %product.1 = (f32[1024,128]{1,0:T(8,128)S(1)}, f32[1024,128]{1,0:T(8,128)S(1)}) custom-call(s32[4]{0:T(128)S(1)} %pad_add_fusion.pos_ref, f32[2,2,128,128]{3,2,1,0:T(8,128)S(1)} %get-tuple-element.28.refs_0_, f32[2,2,128,128]{3,2,1,0:T(8,128)S(1)} %copy-done.5, f32[2,2,2,128,128]{4,3,2,1,0:T(8,128)S(1)} %collective-permute-done.4.refs_2_, ...), custom_call_target="tpu_custom_call" | custom-call | flops 3221225472 | bytes 7340032 | tf_op jit(solution)/shard_map/product/pallas_call | solution.py:214
  81.4 0.1 collective-permute-start.21
  81.5 1.9 %collective-permute-done.21 = f32[1024,128]{1,0:T(8,128)S(1)} collective-permute-done((f32[1024,128]{1,0:T(8,128)S(1)}, f32[1024,128]{1,0:T(8,128)S(1)}, u32[]{:S(2)}, u32[]{:S(2)}) %collective-permute-start.21) | collective-permute-done | bytes 524320 | tf_op jit(solution)/shard_map/ppermute | solution.py:20
  83.4 0.0 copy-done
  83.4 1.7 %finish.1 = f32[16,128,128]{2,1,0:T(8,128)} custom-call(s32[4]{0:T(128)S(1)} %pad_add_fusion.pos_ref, f32[16,128,128]{2,1,0:T(8,128)S(1)} %bitcast.28, f32[8,128,128]{2,1,0:T(8,128)S(1)} %bitcast.29, f32[8,128,128]{2,1,0:T(8,128)S(1)} %bitcast.30), custom_call_target="tpu_custom_call" | custom-call | bytes 3145728 | tf_op jit(solution)/shard_map/finish/pallas_call | solution.py:234
  (9 shorter events, 0.2 us)
Async XLA Ops:
  1.0 7.8 %collective-permute-start.7 = (f32[2,128,128]{2,1,0:T(8,128)S(1)}, f32[2,128,128]{2,1,0:T(8,128)S(1)}, u32[]{:S(2)}, u32[]{:S(2)}) collective-permute-start(f32[2,128,128]{2,1,0:T(8,128)S(1)} %bitcast.34), channel_id=1, source_target_pairs={{0,4},{4,0},{1,5},{5,1},{2,6},{6,2},{3,7},{7,3},{8,12},{12,8},{9,1... | collective-permute-start | bytes 393224 | tf_op jit(solution)/shard_map/ppermute | solution.py:20
  4.3 10.1 %collective-permute-start = (f32[2,128,128]{2,1,0:T(8,128)S(1)}, f32[2,128,128]{2,1,0:T(8,128)S(1)}, u32[]{:S(2)}, u32[]{:S(2)}) collective-permute-start(f32[2,128,128]{2,1,0:T(8,128)S(1)} %bitcast.35), channel_id=1, source_target_pairs={{0,0},{4,1},{8,2},{12,3},{16,4},{20,5},{24,6},{28,7},{2,8},{6,9},{... | collective-permute-start | bytes 393224 | tf_op jit(solution)/shard_map/ppermute | solution.py:30
  6.3 8.3 %collective-permute-start.1 = (f32[2,128,128]{2,1,0:T(8,128)S(1)}, f32[2,128,128]{2,1,0:T(8,128)S(1)}, u32[]{:S(2)}, u32[]{:S(2)}) collective-permute-start(f32[2,128,128]{2,1,0:T(8,128)S(1)} %bitcast.36), channel_id=1, source_target_pairs={{1,0},{5,1},{9,2},{13,3},{17,4},{21,5},{25,6},{29,7},{3,8},{7,9},{... | collective-permute-start | bytes 393224 | tf_op jit(solution)/shard_map/ppermute | solution.py:30
  8.9 10.7 %collective-permute-start.8 = (f32[2,128,128]{2,1,0:T(8,128)S(1)}, f32[2,128,128]{2,1,0:T(8,128)S(1)}, u32[]{:S(2)}, u32[]{:S(2)}) collective-permute-start(f32[2,128,128]{2,1,0:T(8,128)S(1)} %slice_select_fusion), channel_id=1, source_target_pairs={{0,132},{4,68},{1,133},{5,69},{2,134},{6,70},{3,135},{7,71},{8,140... | collective-permute-start | bytes 393224 | tf_op jit(solution)/shard_map/ppermute | solution.py:263
  13.8 5.8 %collective-permute-start.9 = (f32[2,128,128]{2,1,0:T(8,128)S(1)}, f32[2,128,128]{2,1,0:T(8,128)S(1)}, u32[]{:S(2)}, u32[]{:S(2)}) collective-permute-start(f32[2,128,128]{2,1,0:T(8,128)S(1)} %slice_select_fusion), channel_id=1, source_target_pairs={{0,196},{1,197},{2,198},{3,199},{8,204},{9,205},{10,206},{11,207},... | collective-permute-start | bytes 393224 | tf_op jit(solution)/shard_map/ppermute | solution.py:263
  14.6 6.1 %collective-permute-start.3 = (f32[2,2,128,128]{3,2,1,0:T(8,128)S(1)}, f32[2,2,128,128]{3,2,1,0:T(8,128)S(1)}, u32[]{:S(2)}, u32[]{:S(2)}) collective-permute-start(f32[2,2,128,128]{3,2,1,0:T(8,128)S(1)} %get-tuple-element.28.refs_0_), channel_id=1, source_target_pairs={{0,4},{4,0},{1,5},{5,1},{2,6},{6,2},{3,7},{7,3},{8,12},{12,8},{9,1... | collective-permute-start | bytes 786440 | tf_op jit(solution)/shard_map/ppermute | solution.py:20
  19.6 2.5 %collective-permute-start.10 = (f32[2,128,128]{2,1,0:T(8,128)S(1)}, f32[2,128,128]{2,1,0:T(8,128)S(1)}, u32[]{:S(2)}, u32[]{:S(2)}) collective-permute-start(f32[2,128,128]{2,1,0:T(8,128)S(1)} %select_select_fusion), channel_id=1, source_target_pairs={{0,36},{68,100},{132,164},{196,228},{1,37},{69,101},{133,165},{197... | collective-permute-start | bytes 393224 | tf_op jit(solution)/shard_map/ppermute | solution.py:263
  20.7 14.4 %collective-permute-start.4 = (f32[2,2,2,128,128]{4,3,2,1,0:T(8,128)S(1)}, f32[2,2,2,128,128]{4,3,2,1,0:T(8,128)S(1)}, u32[]{:S(2)}, u32[]{:S(2)}) collective-permute-start(f32[2,2,2,128,128]{4,3,2,1,0:T(8,128)S(1)} %pad_maximum_fusion.1), channel_id=1, source_target_pairs={{0,32},{32,64},{64,96},{96,128},{128,160},{160,192},{192,224},{224... | collective-permute-start | bytes 1572872 | tf_op jit(solution)/shard_map/ppermute | solution.py:253
  22.1 8.9 %collective-permute-start.11 = (f32[2,128,128]{2,1,0:T(8,128)S(1)}, f32[2,128,128]{2,1,0:T(8,128)S(1)}, u32[]{:S(2)}, u32[]{:S(2)}) collective-permute-start(f32[2,128,128]{2,1,0:T(8,128)S(1)} %broadcast_select_fusion), channel_id=1, source_target_pairs={{4,12},{12,4},{20,28},{28,20},{5,13},{13,5},{21,29},{29,21},{6,14}... | collective-permute-start | bytes 393224 | tf_op jit(solution)/shard_map/ppermute | solution.py:272
  28.1 6.3 %collective-permute-start.2 = (f32[2,2,128,128]{3,2,1,0:T(8,128)S(1)}, f32[2,2,128,128]{3,2,1,0:T(8,128)S(1)}, u32[]{:S(2)}, u32[]{:S(2)}) collective-permute-start(f32[2,2,128,128]{3,2,1,0:T(8,128)S(1)} %get-tuple-element.28.refs_0_), channel_id=1, source_target_pairs={{0,8},{8,16},{16,24},{24,0},{4,28},{12,4},{20,12},{28,20},{1,9},{9... | collective-permute-start | bytes 786440 | tf_op jit(solution)/shard_map/ppermute | solution.py:253
  31.0 14.1 %collective-permute-start.16 = (f32[4,128,128]{2,1,0:T(8,128)S(1)}, f32[4,128,128]{2,1,0:T(8,128)S(1)}, u32[]{:S(2)}, u32[]{:S(2)}) collective-permute-start(f32[4,128,128]{2,1,0:T(8,128)S(1)} %maximum_select_fusion.1.q0), channel_id=1, source_target_pairs={{0,1},{1,2},{2,3},{3,0},{4,5},{5,6},{6,7},{7,4},{8,9},{9,10},{10,1... | collective-permute-start | bytes 786440 | tf_op jit(solution)/shard_map/ppermute | solution.py:16
  31.9 13.2 %collective-permute-start.17 = (f32[4,128,128]{2,1,0:T(8,128)S(1)}, f32[4,128,128]{2,1,0:T(8,128)S(1)}, u32[]{:S(2)}, u32[]{:S(2)}) collective-permute-start(f32[4,128,128]{2,1,0:T(8,128)S(1)} %maximum_select_fusion.1.q0), channel_id=1, source_target_pairs={{0,2},{1,3},{2,0},{3,1},{4,6},{5,7},{6,4},{7,5},{8,10},{9,11},{10,... | collective-permute-start | bytes 786440 | tf_op jit(solution)/shard_map/ppermute | solution.py:16
  33.9 11.3 %collective-permute-start.18 = (f32[4,128,128]{2,1,0:T(8,128)S(1)}, f32[4,128,128]{2,1,0:T(8,128)S(1)}, u32[]{:S(2)}, u32[]{:S(2)}) collective-permute-start(f32[4,128,128]{2,1,0:T(8,128)S(1)} %maximum_select_fusion.1.q0), channel_id=1, source_target_pairs={{0,3},{1,0},{2,1},{3,2},{4,7},{5,4},{6,5},{7,6},{8,11},{9,8},{10,9... | collective-permute-start | bytes 786440 | tf_op jit(solution)/shard_map/ppermute | solution.py:16
  34.4 0.7 copy-start.4
  35.1 11.1 %collective-permute-start.5 = (f32[2,2,2,128,128]{4,3,2,1,0:T(8,128)S(1)}, f32[2,2,2,128,128]{4,3,2,1,0:T(8,128)S(1)}, u32[]{:S(2)}, u32[]{:S(2)}) collective-permute-start(f32[2,2,2,128,128]{4,3,2,1,0:T(8,128)S(1)} %collective-permute-done.4.refs_2_), channel_id=1, source_target_pairs={{0,8},{8,16},{16,24},{24,0},{4,28},{12,4},{20,12},{28,20},{1,9},{9... | collective-permute-start | bytes 1572872 | tf_op jit(solution)/shard_map/ppermute | solution.py:253
  39.5 11.8 %collective-permute-start.6 = (f32[2,2,2,128,128]{4,3,2,1,0:T(8,128)S(1)}, f32[2,2,2,128,128]{4,3,2,1,0:T(8,128)}, u32[]{:S(2)}, u32[]{:S(2)}) collective-permute-start(f32[2,2,2,128,128]{4,3,2,1,0:T(8,128)S(1)} %collective-permute-done.4.refs_2_), channel_id=1, source_target_pairs={{0,32},{32,64},{64,96},{96,128},{128,160},{160,192},{192,224},{224... | collective-permute-start | bytes 1572872 | tf_op jit(solution)/shard_map/ppermute | solution.py:253
  46.2 18.5 %collective-permute-start.19 = (f32[4,4,128,128]{3,2,1,0:T(8,128)}, f32[4,4,128,128]{3,2,1,0:T(8,128)S(1)}, u32[]{:S(2)}, u32[]{:S(2)}) collective-permute-start(f32[4,4,128,128]{3,2,1,0:T(8,128)} %pad_maximum_fusion), channel_id=1, source_target_pairs={{0,4},{4,0},{1,5},{5,1},{2,6},{6,2},{3,7},{7,3},{8,12},{12,8},{9,1... | collective-permute-start | bytes 3145736 | tf_op jit(solution)/shard_map/ppermute | solution.py:20
  46.2 0.8 copy-start.2
  51.2 9.7 %collective-permute-start.13 = (f32[2,2,2,128,128]{4,3,2,1,0:T(8,128)}, f32[2,2,2,128,128]{4,3,2,1,0:T(8,128)S(1)}, u32[]{:S(2)}, u32[]{:S(2)}) collective-permute-start(f32[2,2,2,128,128]{4,3,2,1,0:T(8,128)} %collective-permute-done.6.refs_4_), channel_id=1, source_target_pairs={{0,32},{32,64},{64,96},{96,128},{128,160},{160,192},{192,224},{224... | collective-permute-start | bytes 1572872 | tf_op jit(solution)/shard_map/ppermute | solution.py:253
  54.4 8.5 %collective-permute-start.12 = (f32[2,2,2,128,128]{4,3,2,1,0:T(8,128)}, f32[2,2,2,128,128]{4,3,2,1,0:T(8,128)}, u32[]{:S(2)}, u32[]{:S(2)}) collective-permute-start(f32[2,2,2,128,128]{4,3,2,1,0:T(8,128)} %collective-permute-done.6.refs_4_), channel_id=1, source_target_pairs={{0,8},{8,16},{16,24},{24,0},{4,28},{12,4},{20,12},{28,20},{1,9},{9... | collective-permute-start | bytes 1572872 | tf_op jit(solution)/shard_map/ppermute | solution.py:253
  60.9 17.3 %copy-start.3 = (f32[2,2,2,128,128]{4,3,2,1,0:T(8,128)S(1)}, f32[2,2,2,128,128]{4,3,2,1,0:T(8,128)}, u32[]{:S(2)}) copy-start(f32[2,2,2,128,128]{4,3,2,1,0:T(8,128)} %copy-done.2) | copy-start | bytes 1572868
  63.0 9.9 %collective-permute-start.15 = (f32[2,2,128,128]{3,2,1,0:T(8,128)S(1)}, f32[2,2,128,128]{3,2,1,0:T(8,128)S(1)}, u32[]{:S(2)}, u32[]{:S(2)}) collective-permute-start(f32[2,2,128,128]{3,2,1,0:T(8,128)S(1)} %slice_bitcast_fusion), channel_id=1, source_target_pairs={{0,32},{32,64},{64,96},{96,128},{128,160},{160,192},{192,224},{224... | collective-permute-start | bytes 786440 | tf_op jit(solution)/shard_map/ppermute | solution.py:253
  64.0 14.2 %collective-permute-start.14 = (f32[2,2,2,128,128]{4,3,2,1,0:T(8,128)S(1)}, f32[2,2,2,128,128]{4,3,2,1,0:T(8,128)S(1)}, u32[]{:S(2)}, u32[]{:S(2)}) collective-permute-start(f32[2,2,2,128,128]{4,3,2,1,0:T(8,128)S(1)} %collective-permute-done.13.refs_6_), channel_id=1, source_target_pairs={{0,8},{8,16},{16,24},{24,0},{4,28},{12,4},{20,12},{28,20},{1,9},{9... | collective-permute-start | bytes 1572872 | tf_op jit(solution)/shard_map/ppermute | solution.py:253
  64.7 1.6 %copy-start.1 = (f32[2,512,512]{2,1,0:T(8,128)S(1)}, f32[2,512,512]{2,1,0:T(8,128)}, u32[]{:S(2)}) copy-start(f32[2,512,512]{2,1,0:T(8,128)} %l_ref.1) | copy-start | bytes 6291460
  66.3 11.9 %copy-start.5 = (f32[2,2,128,128]{3,2,1,0:T(8,128)S(1)}, f32[2,2,128,128]{3,2,1,0:T(8,128)}, u32[]{:S(2)}) copy-start(f32[2,2,128,128]{3,2,1,0:T(8,128)} %copy-done.4) | copy-start | bytes 786436
  72.9 10.5 %copy-start = (f32[16,128,1,128]{3,2,1,0:T(1,128)S(1)}, f32[16,128,1,128]{3,2,1,0:T(1,128)}, u32[]{:S(2)}) copy-start(f32[16,128,1,128]{3,2,1,0:T(1,128)} %param.2) | copy-start | bytes 3145732
  72.9 5.3 %collective-permute-start.20 = (f32[2,2,128,128]{3,2,1,0:T(8,128)S(1)}, f32[2,2,128,128]{3,2,1,0:T(8,128)S(1)}, u32[]{:S(2)}, u32[]{:S(2)}) collective-permute-start(f32[2,2,128,128]{3,2,1,0:T(8,128)S(1)} %collective-permute-done.15.refs_8_), channel_id=1, source_target_pairs={{0,8},{8,16},{16,24},{24,0},{4,28},{12,4},{20,12},{28,20},{1,9},{9... | collective-permute-start | bytes 786440 | tf_op jit(solution)/shard_map/ppermute | solution.py:253
  81.4 2.0 %collective-permute-start.21 = (f32[1024,128]{1,0:T(8,128)S(1)}, f32[1024,128]{1,0:T(8,128)S(1)}, u32[]{:S(2)}, u32[]{:S(2)}) collective-permute-start(f32[1024,128]{1,0:T(8,128)S(1)} %get-tuple-element.26), channel_id=1, source_target_pairs={{0,4},{4,0},{1,5},{5,1},{2,6},{6,2},{3,7},{7,3},{8,12},{12,8},{9,1... | collective-permute-start | bytes 1572872 | tf_op jit(solution)/shard_map/ppermute | solution.py:20

commit v3 on v2

--- a/solution.py
+++ b/solution.py
@@ -272,13 +272,13 @@
     beside = lax.ppermute(corner, ("x", "k"), [(2 * i + 1, 2 * (i ^ 1) + 1) for i in range(X)])
     gathered = gather_y(jnp.where(k == 0, columns, jnp.concatenate([corner, beside])))
 
-    r2 = around(after(r1, s0), "z", Z)
-    s1 = around(after(r1, s0), "x", X)
-    r3 = around(after(r2, s1, gathered[0]), "z", Z)
-    s2 = around(after(r2, s1, gathered[0]), "x", X)
+    r2 = around(r1, "z", Z)
+    s1 = around(r1, "x", X)
+    r3 = around(r2, "z", Z)
+    s2 = around(r2, "x", X)
     zs = factor(pos, inverse_factors, gathered, other_core(jnp.stack(gathered)))
-    r4 = around(after(r3[0], s2), "z", Z)
-    s3 = around(after(r3, s2), "x", X)
+    r4 = around(r3[0], "z", Z)
+    s3 = around(r3, "x", X)
     s4 = around(after(r4, *zs), "x", X)
 
     def piece(ring, side, *at):

time: 85.3 us -> 83.8 us (0.982)
  local copies, waits for them, and re-layouts: 4.17 us -> 2.62 us
  starting transfers between devices: 47.9 us -> 48.8 us
    ppermute x9, waiting for transfers between devices: 17.1 us -> 13.4 us  [around(): return lax.ppermute(v, (axis, 'k'), perm)]
    ppermute x1, waiting for transfers between devices: 0.42 us -> 2.64 us  [shards(): lax.ppermute(corner, ('x', 'k'), [(2 * i + 1, 2 * (i ^ 1) + 1) for i in r...]
    unnamed x13 -> x5, local copies, waits for them, and re-layouts: 3.24 us -> 1.69 us
where the time goes in v3:
time: 83.8 us; the launch traced here: 83.5 us
  starting transfers between devices  48.8 us (58%)
  waiting for transfers between devices  19.3 us (23%)
  Pallas kernels  11.3 us (13%)
  local copies, waits for them, and re-layouts  2.62 us (3%)
  other arithmetic  1.33 us (2%)
    ppermute x9, starting transfers between devices, around(): return lax.ppermute(v, (axis, 'k'), perm)  20.4 us
    ppermute x9, waiting for transfers between devices, around(): return lax.ppermute(v, (axis, 'k'), perm)  13.4 us
    ppermute x4, starting transfers between devices, other_core(): return lax.ppermute(v, 'k', [(0, 1), (1, 0)])  8.33 us
    pallas_call x1, Pallas kernels, factor(): pl.pallas_call(body, out_shape=(Z16, Z16, WIDE16, WIDE16), in_specs=[SMEM...  6.52 us
    ppermute x3, starting transfers between devices, to_core1(): lax.ppermute(v, ('z', 'k'), [(2 * i + c, 2 * j + 1) for i, c, j in pairs])  6.24 us
    ppermute x1, starting transfers between devices, shards(): lax.ppermute(corner, ('x', 'k'), [(2 * i + 1, 2 * (i ^ 1) + 1) for i in r...  5.91 us
    ppermute x2, starting transfers between devices, swap(): return lax.ppermute(v, ('x', 'k', 'y'), perm)  4.45 us
    ppermute x3, starting transfers between devices, shift(): return lax.ppermute(v, axis, [(i, (i + step) % size) for i in range(size)])  3.52 us
  transfers between devices with their start and end apart: 22, of which 8 were waited for; matrix products, arithmetic and copies ran while one was open for 2% of the time, Pallas kernels for 8%

profile of v3, /device:TPU:1, one launch (start us, length us, event | category | flops | bytes accessed | tf_op | source)
XLA Modules:
  0.0 83.5 jit_solution(7888919691190343271)
XLA Ops:
  0.0 0.9 %slice.15 = f32[2,128,1,128]{3,2,1,0:T(1,128)S(1)} slice(f32[16,128,1,128]{3,2,1,0:T(1,128)} %param.2), slice={[0:2], [0:128], [0:1], [0:128]} | slice | bytes 262144 | tf_op jit(solution)/shard_map/slice | solution.py:255
  0.9 0.1 copy.5
  1.0 3.3 %collective-permute-start.11 = (f32[2,128,128]{2,1,0:T(8,128)S(1)}, f32[2,128,128]{2,1,0:T(8,128)S(1)}, u32[]{:S(2)}, u32[]{:S(2)}) collective-permute-start(f32[2,128,128]{2,1,0:T(8,128)S(1)} %bitcast.34), channel_id=1, source_target_pairs={{0,4},{4,0},{1,5},{5,1},{2,6},{6,2},{3,7},{7,3},{8,12},{12,8},{9,1... | collective-permute-start | bytes 393224 | tf_op jit(solution)/shard_map/ppermute | solution.py:20
  4.3 1.9 %collective-permute-start = (f32[2,128,128]{2,1,0:T(8,128)S(1)}, f32[2,128,128]{2,1,0:T(8,128)S(1)}, u32[]{:S(2)}, u32[]{:S(2)}) collective-permute-start(f32[2,128,128]{2,1,0:T(8,128)S(1)} %bitcast.35), channel_id=1, source_target_pairs={{0,0},{4,1},{8,2},{12,3},{16,4},{20,5},{24,6},{28,7},{2,8},{6,9},{... | collective-permute-start | bytes 393224 | tf_op jit(solution)/shard_map/ppermute | solution.py:30
  6.3 2.5 %collective-permute-start.1 = (f32[2,128,128]{2,1,0:T(8,128)S(1)}, f32[2,128,128]{2,1,0:T(8,128)S(1)}, u32[]{:S(2)}, u32[]{:S(2)}) collective-permute-start(f32[2,128,128]{2,1,0:T(8,128)S(1)} %bitcast.36), channel_id=1, source_target_pairs={{1,0},{5,1},{9,2},{13,3},{17,4},{21,5},{25,6},{29,7},{3,8},{7,9},{... | collective-permute-start | bytes 393224 | tf_op jit(solution)/shard_map/ppermute | solution.py:30
  8.8 0.0 collective-permute-done.11
  8.9 4.9 %collective-permute-start.12 = (f32[2,128,128]{2,1,0:T(8,128)S(1)}, f32[2,128,128]{2,1,0:T(8,128)S(1)}, u32[]{:S(2)}, u32[]{:S(2)}) collective-permute-start(f32[2,128,128]{2,1,0:T(8,128)S(1)} %slice_select_fusion), channel_id=1, source_target_pairs={{0,132},{4,68},{1,133},{5,69},{2,134},{6,70},{3,135},{7,71},{8,140... | collective-permute-start | bytes 393224 | tf_op jit(solution)/shard_map/ppermute | solution.py:263
  13.8 0.7 collective-permute-start.13
  14.4 0.0 collective-permute-done
  14.5 0.1 collective-permute-done.1
  14.6 4.9 %collective-permute-start.3 = (f32[2,2,128,128]{3,2,1,0:T(8,128)S(1)}, f32[2,2,128,128]{3,2,1,0:T(8,128)S(1)}, u32[]{:S(2)}, u32[]{:S(2)}) collective-permute-start(f32[2,2,128,128]{3,2,1,0:T(8,128)S(1)} %get-tuple-element.20.refs_0_), channel_id=1, source_target_pairs={{0,4},{4,0},{1,5},{5,1},{2,6},{6,2},{3,7},{7,3},{8,12},{12,8},{9,1... | collective-permute-start | bytes 786440 | tf_op jit(solution)/shard_map/ppermute | solution.py:20
  19.5 0.0 collective-permute-done.12
  19.5 0.0 collective-permute-done.13
  19.6 0.7 collective-permute-start.14
  20.3 0.4 collective-permute-done.3
  20.7 1.4 %collective-permute-start.4 = (f32[2,2,2,128,128]{4,3,2,1,0:T(8,128)S(1)}, f32[2,2,2,128,128]{4,3,2,1,0:T(8,128)S(1)}, u32[]{:S(2)}, u32[]{:S(2)}) collective-permute-start(f32[2,2,2,128,128]{4,3,2,1,0:T(8,128)S(1)} %pad_maximum_fusion.1), channel_id=1, source_target_pairs={{0,32},{32,64},{64,96},{96,128},{128,160},{160,192},{192,224},{224... | collective-permute-start | bytes 1572872 | tf_op jit(solution)/shard_map/ppermute | solution.py:253
  22.1 0.0 collective-permute-done.14
  22.1 5.9 %collective-permute-start.15 = (f32[2,128,128]{2,1,0:T(8,128)S(1)}, f32[2,128,128]{2,1,0:T(8,128)S(1)}, u32[]{:S(2)}, u32[]{:S(2)}) collective-permute-start(f32[2,128,128]{2,1,0:T(8,128)S(1)} %broadcast_select_fusion), channel_id=1, source_target_pairs={{4,12},{12,4},{20,28},{28,20},{5,13},{13,5},{21,29},{29,21},{6,14}... | collective-permute-start | bytes 393224 | tf_op jit(solution)/shard_map/ppermute | solution.py:272
  28.1 2.6 %collective-permute-done.15 = f32[2,128,128]{2,1,0:T(8,128)S(1)} collective-permute-done((f32[2,128,128]{2,1,0:T(8,128)S(1)}, f32[2,128,128]{2,1,0:T(8,128)S(1)}, u32[]{:S(2)}, u32[]{:S(2)}) %collective-permute-start.15) | collective-permute-done | bytes 131104 | tf_op jit(solution)/shard_map/ppermute | solution.py:272
  30.7 1.0 %collective-permute-start.16 = (f32[4,128,128]{2,1,0:T(8,128)S(1)}, f32[4,128,128]{2,1,0:T(8,128)S(1)}, u32[]{:S(2)}, u32[]{:S(2)}) collective-permute-start(f32[4,128,128]{2,1,0:T(8,128)S(1)} %maximum_select_fusion.1.q0), channel_id=1, source_target_pairs={{0,1},{1,2},{2,3},{3,0},{4,5},{5,6},{6,7},{7,4},{8,9},{9,10},{10,1... | collective-permute-start | bytes 786440 | tf_op jit(solution)/shard_map/ppermute | solution.py:16
  31.8 2.1 %collective-permute-start.17 = (f32[4,128,128]{2,1,0:T(8,128)S(1)}, f32[4,128,128]{2,1,0:T(8,128)S(1)}, u32[]{:S(2)}, u32[]{:S(2)}) collective-permute-start(f32[4,128,128]{2,1,0:T(8,128)S(1)} %maximum_select_fusion.1.q0), channel_id=1, source_target_pairs={{0,2},{1,3},{2,0},{3,1},{4,6},{5,7},{6,4},{7,5},{8,10},{9,11},{10,... | collective-permute-start | bytes 786440 | tf_op jit(solution)/shard_map/ppermute | solution.py:16
  33.9 0.4 collective-permute-start.18
  34.3 0.0 collective-permute-done.4.refs_2_
  34.3 8.2 %collective-permute-start.6 = (f32[2,2,2,128,128]{4,3,2,1,0:T(8,128)S(1)}, f32[2,2,2,128,128]{4,3,2,1,0:T(8,128)}, u32[]{:S(2)}, u32[]{:S(2)}) collective-permute-start(f32[2,2,2,128,128]{4,3,2,1,0:T(8,128)S(1)} %collective-permute-done.4.refs_2_), channel_id=1, source_target_pairs={{0,32},{32,64},{64,96},{96,128},{128,160},{160,192},{192,224},{224... | collective-permute-start | bytes 1572872 | tf_op jit(solution)/shard_map/ppermute | solution.py:253
  42.4 0.0 collective-permute-done.16.q1
  42.5 0.7 collective-permute-done.17.q2
  43.2 0.0 collective-permute-done.18.q3
  43.2 1.0 %pad_maximum_fusion = f32[4,4,128,128]{3,2,1,0:T(8,128)} fusion(f32[1,4,128,128]{3,2,1,0:T(8,128)S(1)} %bitcast.33, f32[1,4,128,128]{3,2,1,0:T(8,128)S(1)} %bitcast.32, f32[1,4,128,128]{3,2,1,0:T(8,128)S(1)} %bitcast.31, f32[1,4,128,128]{3,2,1,0:T(8,128)S(1)} %fusion), kind=kLoop, calls=%fused_computation | loop fusion | flops 786432 | bytes 2097152 | tf_op jit(solution)/shard_map/stack | solution.py:279
  44.2 0.0 collective-permute-start.19
  44.2 4.3 %collective-permute-done.6.refs_4_ = f32[2,2,2,128,128]{4,3,2,1,0:T(8,128)} collective-permute-done((f32[2,2,2,128,128]{4,3,2,1,0:T(8,128)S(1)}, f32[2,2,2,128,128]{4,3,2,1,0:T(8,128)}, u32[]{:S(2)}, u32[]{:S(2)}) %collective-permute-start.6) | collective-permute-done | bytes 524320 | tf_op jit(solution)/shard_map/ppermute | solution.py:253
  48.5 3.2 %collective-permute-start.8 = (f32[2,2,2,128,128]{4,3,2,1,0:T(8,128)}, f32[2,2,2,128,128]{4,3,2,1,0:T(8,128)S(1)}, u32[]{:S(2)}, u32[]{:S(2)}) collective-permute-start(f32[2,2,2,128,128]{4,3,2,1,0:T(8,128)} %collective-permute-done.6.refs_4_), channel_id=1, source_target_pairs={{0,32},{32,64},{64,96},{96,128},{128,160},{160,192},{192,224},{224... | collective-permute-start | bytes 1572872 | tf_op jit(solution)/shard_map/ppermute | solution.py:253
  51.8 0.1 pad_add_fusion.pos_ref
  51.8 2.0 %collective-permute-start.2 = (f32[2,2,128,128]{3,2,1,0:T(8,128)S(1)}, f32[2,2,128,128]{3,2,1,0:T(8,128)S(1)}, u32[]{:S(2)}, u32[]{:S(2)}) collective-permute-start(f32[2,2,128,128]{3,2,1,0:T(8,128)S(1)} %get-tuple-element.20.refs_0_), channel_id=1, source_target_pairs={{0,8},{8,16},{16,24},{24,0},{4,28},{12,4},{20,12},{28,20},{1,9},{9... | collective-permute-start | bytes 786440 | tf_op jit(solution)/shard_map/ppermute | solution.py:253
  53.8 0.1 collective-permute-start.5
  53.9 0.3 collective-permute-start.7
  54.2 4.0 %collective-permute-done.8.refs_6_ = f32[2,2,2,128,128]{4,3,2,1,0:T(8,128)S(1)} collective-permute-done((f32[2,2,2,128,128]{4,3,2,1,0:T(8,128)}, f32[2,2,2,128,128]{4,3,2,1,0:T(8,128)S(1)}, u32[]{:S(2)}, u32[]{:S(2)}) %collective-permute-start.8) | collective-permute-done | bytes 524320 | tf_op jit(solution)/shard_map/ppermute | solution.py:253
  58.2 3.4 %collective-permute-start.10 = (f32[2,2,128,128]{3,2,1,0:T(8,128)S(1)}, f32[2,2,128,128]{3,2,1,0:T(8,128)S(1)}, u32[]{:S(2)}, u32[]{:S(2)}) collective-permute-start(f32[2,2,128,128]{3,2,1,0:T(8,128)S(1)} %slice_bitcast_fusion), channel_id=1, source_target_pairs={{0,32},{32,64},{64,96},{96,128},{128,160},{160,192},{192,224},{224... | collective-permute-start | bytes 786440 | tf_op jit(solution)/shard_map/ppermute | solution.py:253
  61.6 0.0 collective-permute-done.19.got_ref
  61.6 1.7 %collective-permute-start.9 = (f32[2,2,2,128,128]{4,3,2,1,0:T(8,128)S(1)}, f32[2,2,2,128,128]{4,3,2,1,0:T(8,128)S(1)}, u32[]{:S(2)}, u32[]{:S(2)}) collective-permute-start(f32[2,2,2,128,128]{4,3,2,1,0:T(8,128)S(1)} %collective-permute-done.8.refs_6_), channel_id=1, source_target_pairs={{0,8},{8,16},{16,24},{24,0},{4,28},{12,4},{20,12},{28,20},{1,9},{9... | collective-permute-start | bytes 1572872 | tf_op jit(solution)/shard_map/ppermute | solution.py:253
  63.3 0.0 copy-start.1
  63.3 1.6 %copy-done.1 = f32[2,512,512]{2,1,0:T(8,128)S(1)} copy-done((f32[2,512,512]{2,1,0:T(8,128)S(1)}, f32[2,512,512]{2,1,0:T(8,128)}, u32[]{:S(2)}) %copy-start.1) | copy-done | bytes 2097176
  64.9 6.5 %factor.1 = (bf16[256,1024]{1,0:T(8,128)(2,1)S(1)}, bf16[256,1024]{1,0:T(8,128)(2,1)S(1)}, bf16[256,512]{1,0:T(8,128)(2,1)S(1)}, bf16[256,512]{1,0:T(8,128)(2,1)S(1)}) custom-call(s32[4]{0:T(128)S(1)} %pad_add_fusion.pos_ref, f32[2,512,512]{2,1,0:T(8,128)S(1)} %copy-done.1, f32[4,128,128]{2,1,0:T(8,128)S(1)} %maximum_select_fusion.1.q0, ...), custom_call_target="tpu_custom_call" | custom-call | flops 3221225472 | bytes 6291456 | tf_op jit(solution)/shard_map/factor/pallas_call | solution.py:148
  71.4 0.0 collective-permute-done.10.refs_8_
  71.4 0.0 copy-start
  71.4 0.2 collective-permute-start.20
  71.6 0.0 collective-permute-done.2.refs_1_
  71.6 0.0 collective-permute-done.5.refs_3_
  71.6 0.0 collective-permute-done.7.refs_5_
  71.6 5.2 %collective-permute-done.20.refs_9_ = f32[2,2,128,128]{3,2,1,0:T(8,128)S(1)} collective-permute-done((f32[2,2,128,128]{3,2,1,0:T(8,128)S(1)}, f32[2,2,128,128]{3,2,1,0:T(8,128)S(1)}, u32[]{:S(2)}, u32[]{:S(2)}) %collective-permute-start.20) | collective-permute-done | bytes 262176 | tf_op jit(solution)/shard_map/ppermute | solution.py:253
  76.8 0.0 collective-permute-done.9.refs_7_
  76.8 3.1 %product.1 = (f32[1024,128]{1,0:T(8,128)S(1)}, f32[1024,128]{1,0:T(8,128)S(1)}) custom-call(s32[4]{0:T(128)S(1)} %pad_add_fusion.pos_ref, f32[2,2,128,128]{3,2,1,0:T(8,128)S(1)} %get-tuple-element.20.refs_0_, f32[2,2,128,128]{3,2,1,0:T(8,128)S(1)} %collective-permute-done.2.refs_1_, f32[2,2,2,128,128]{4,3,2,1,0:T(8,128)S(1)} %collective-permute-done.4.refs_2_, ...), custom_call_target="tpu_custom_call" | custom-call | flops 3221225472 | bytes 7340032 | tf_op jit(solution)/shard_map/product/pallas_call | solution.py:214
  79.8 0.1 collective-permute-start.21
  79.9 1.9 %collective-permute-done.21 = f32[1024,128]{1,0:T(8,128)S(1)} collective-permute-done((f32[1024,128]{1,0:T(8,128)S(1)}, f32[1024,128]{1,0:T(8,128)S(1)}, u32[]{:S(2)}, u32[]{:S(2)}) %collective-permute-start.21) | collective-permute-done | bytes 524320 | tf_op jit(solution)/shard_map/ppermute | solution.py:20
  81.8 0.0 copy-done
  81.8 1.7 %finish.1 = f32[16,128,128]{2,1,0:T(8,128)} custom-call(s32[4]{0:T(128)S(1)} %pad_add_fusion.pos_ref, f32[16,128,128]{2,1,0:T(8,128)S(1)} %bitcast.28, f32[8,128,128]{2,1,0:T(8,128)S(1)} %bitcast.29, f32[8,128,128]{2,1,0:T(8,128)S(1)} %bitcast.30), custom_call_target="tpu_custom_call" | custom-call | bytes 3145728 | tf_op jit(solution)/shard_map/finish/pallas_call | solution.py:234
  (9 shorter events, 0.2 us)
Async XLA Ops:
  1.0 7.8 %collective-permute-start.11 = (f32[2,128,128]{2,1,0:T(8,128)S(1)}, f32[2,128,128]{2,1,0:T(8,128)S(1)}, u32[]{:S(2)}, u32[]{:S(2)}) collective-permute-start(f32[2,128,128]{2,1,0:T(8,128)S(1)} %bitcast.34), channel_id=1, source_target_pairs={{0,4},{4,0},{1,5},{5,1},{2,6},{6,2},{3,7},{7,3},{8,12},{12,8},{9,1... | collective-permute-start | bytes 393224 | tf_op jit(solution)/shard_map/ppermute | solution.py:20
  4.3 10.1 %collective-permute-start = (f32[2,128,128]{2,1,0:T(8,128)S(1)}, f32[2,128,128]{2,1,0:T(8,128)S(1)}, u32[]{:S(2)}, u32[]{:S(2)}) collective-permute-start(f32[2,128,128]{2,1,0:T(8,128)S(1)} %bitcast.35), channel_id=1, source_target_pairs={{0,0},{4,1},{8,2},{12,3},{16,4},{20,5},{24,6},{28,7},{2,8},{6,9},{... | collective-permute-start | bytes 393224 | tf_op jit(solution)/shard_map/ppermute | solution.py:30
  6.3 8.3 %collective-permute-start.1 = (f32[2,128,128]{2,1,0:T(8,128)S(1)}, f32[2,128,128]{2,1,0:T(8,128)S(1)}, u32[]{:S(2)}, u32[]{:S(2)}) collective-permute-start(f32[2,128,128]{2,1,0:T(8,128)S(1)} %bitcast.36), channel_id=1, source_target_pairs={{1,0},{5,1},{9,2},{13,3},{17,4},{21,5},{25,6},{29,7},{3,8},{7,9},{... | collective-permute-start | bytes 393224 | tf_op jit(solution)/shard_map/ppermute | solution.py:30
  8.9 10.7 %collective-permute-start.12 = (f32[2,128,128]{2,1,0:T(8,128)S(1)}, f32[2,128,128]{2,1,0:T(8,128)S(1)}, u32[]{:S(2)}, u32[]{:S(2)}) collective-permute-start(f32[2,128,128]{2,1,0:T(8,128)S(1)} %slice_select_fusion), channel_id=1, source_target_pairs={{0,132},{4,68},{1,133},{5,69},{2,134},{6,70},{3,135},{7,71},{8,140... | collective-permute-start | bytes 393224 | tf_op jit(solution)/shard_map/ppermute | solution.py:263
  13.8 5.8 %collective-permute-start.13 = (f32[2,128,128]{2,1,0:T(8,128)S(1)}, f32[2,128,128]{2,1,0:T(8,128)S(1)}, u32[]{:S(2)}, u32[]{:S(2)}) collective-permute-start(f32[2,128,128]{2,1,0:T(8,128)S(1)} %slice_select_fusion), channel_id=1, source_target_pairs={{0,196},{1,197},{2,198},{3,199},{8,204},{9,205},{10,206},{11,207},... | collective-permute-start | bytes 393224 | tf_op jit(solution)/shard_map/ppermute | solution.py:263
  14.6 6.1 %collective-permute-start.3 = (f32[2,2,128,128]{3,2,1,0:T(8,128)S(1)}, f32[2,2,128,128]{3,2,1,0:T(8,128)S(1)}, u32[]{:S(2)}, u32[]{:S(2)}) collective-permute-start(f32[2,2,128,128]{3,2,1,0:T(8,128)S(1)} %get-tuple-element.20.refs_0_), channel_id=1, source_target_pairs={{0,4},{4,0},{1,5},{5,1},{2,6},{6,2},{3,7},{7,3},{8,12},{12,8},{9,1... | collective-permute-start | bytes 786440 | tf_op jit(solution)/shard_map/ppermute | solution.py:20
  19.6 2.5 %collective-permute-start.14 = (f32[2,128,128]{2,1,0:T(8,128)S(1)}, f32[2,128,128]{2,1,0:T(8,128)S(1)}, u32[]{:S(2)}, u32[]{:S(2)}) collective-permute-start(f32[2,128,128]{2,1,0:T(8,128)S(1)} %select_select_fusion), channel_id=1, source_target_pairs={{0,36},{68,100},{132,164},{196,228},{1,37},{69,101},{133,165},{197... | collective-permute-start | bytes 393224 | tf_op jit(solution)/shard_map/ppermute | solution.py:263
  20.7 13.5 %collective-permute-start.4 = (f32[2,2,2,128,128]{4,3,2,1,0:T(8,128)S(1)}, f32[2,2,2,128,128]{4,3,2,1,0:T(8,128)S(1)}, u32[]{:S(2)}, u32[]{:S(2)}) collective-permute-start(f32[2,2,2,128,128]{4,3,2,1,0:T(8,128)S(1)} %pad_maximum_fusion.1), channel_id=1, source_target_pairs={{0,32},{32,64},{64,96},{96,128},{128,160},{160,192},{192,224},{224... | collective-permute-start | bytes 1572872 | tf_op jit(solution)/shard_map/ppermute | solution.py:253
  22.1 8.6 %collective-permute-start.15 = (f32[2,128,128]{2,1,0:T(8,128)S(1)}, f32[2,128,128]{2,1,0:T(8,128)S(1)}, u32[]{:S(2)}, u32[]{:S(2)}) collective-permute-start(f32[2,128,128]{2,1,0:T(8,128)S(1)} %broadcast_select_fusion), channel_id=1, source_target_pairs={{4,12},{12,4},{20,28},{28,20},{5,13},{13,5},{21,29},{29,21},{6,14}... | collective-permute-start | bytes 393224 | tf_op jit(solution)/shard_map/ppermute | solution.py:272
  30.7 11.7 %collective-permute-start.16 = (f32[4,128,128]{2,1,0:T(8,128)S(1)}, f32[4,128,128]{2,1,0:T(8,128)S(1)}, u32[]{:S(2)}, u32[]{:S(2)}) collective-permute-start(f32[4,128,128]{2,1,0:T(8,128)S(1)} %maximum_select_fusion.1.q0), channel_id=1, source_target_pairs={{0,1},{1,2},{2,3},{3,0},{4,5},{5,6},{6,7},{7,4},{8,9},{9,10},{10,1... | collective-permute-start | bytes 786440 | tf_op jit(solution)/shard_map/ppermute | solution.py:16
  31.8 11.4 %collective-permute-start.17 = (f32[4,128,128]{2,1,0:T(8,128)S(1)}, f32[4,128,128]{2,1,0:T(8,128)S(1)}, u32[]{:S(2)}, u32[]{:S(2)}) collective-permute-start(f32[4,128,128]{2,1,0:T(8,128)S(1)} %maximum_select_fusion.1.q0), channel_id=1, source_target_pairs={{0,2},{1,3},{2,0},{3,1},{4,6},{5,7},{6,4},{7,5},{8,10},{9,11},{10,... | collective-permute-start | bytes 786440 | tf_op jit(solution)/shard_map/ppermute | solution.py:16
  33.9 9.3 %collective-permute-start.18 = (f32[4,128,128]{2,1,0:T(8,128)S(1)}, f32[4,128,128]{2,1,0:T(8,128)S(1)}, u32[]{:S(2)}, u32[]{:S(2)}) collective-permute-start(f32[4,128,128]{2,1,0:T(8,128)S(1)} %maximum_select_fusion.1.q0), channel_id=1, source_target_pairs={{0,3},{1,0},{2,1},{3,2},{4,7},{5,4},{6,5},{7,6},{8,11},{9,8},{10,9... | collective-permute-start | bytes 786440 | tf_op jit(solution)/shard_map/ppermute | solution.py:16
  34.3 14.3 %collective-permute-start.6 = (f32[2,2,2,128,128]{4,3,2,1,0:T(8,128)S(1)}, f32[2,2,2,128,128]{4,3,2,1,0:T(8,128)}, u32[]{:S(2)}, u32[]{:S(2)}) collective-permute-start(f32[2,2,2,128,128]{4,3,2,1,0:T(8,128)S(1)} %collective-permute-done.4.refs_2_), channel_id=1, source_target_pairs={{0,32},{32,64},{64,96},{96,128},{128,160},{160,192},{192,224},{224... | collective-permute-start | bytes 1572872 | tf_op jit(solution)/shard_map/ppermute | solution.py:253
  44.2 17.4 %collective-permute-start.19 = (f32[4,4,128,128]{3,2,1,0:T(8,128)}, f32[4,4,128,128]{3,2,1,0:T(8,128)S(1)}, u32[]{:S(2)}, u32[]{:S(2)}) collective-permute-start(f32[4,4,128,128]{3,2,1,0:T(8,128)} %pad_maximum_fusion), channel_id=1, source_target_pairs={{0,4},{4,0},{1,5},{5,1},{2,6},{6,2},{3,7},{7,3},{8,12},{12,8},{9,1... | collective-permute-start | bytes 3145736 | tf_op jit(solution)/shard_map/ppermute | solution.py:20
  48.5 9.7 %collective-permute-start.8 = (f32[2,2,2,128,128]{4,3,2,1,0:T(8,128)}, f32[2,2,2,128,128]{4,3,2,1,0:T(8,128)S(1)}, u32[]{:S(2)}, u32[]{:S(2)}) collective-permute-start(f32[2,2,2,128,128]{4,3,2,1,0:T(8,128)} %collective-permute-done.6.refs_4_), channel_id=1, source_target_pairs={{0,32},{32,64},{64,96},{96,128},{128,160},{160,192},{192,224},{224... | collective-permute-start | bytes 1572872 | tf_op jit(solution)/shard_map/ppermute | solution.py:253
  51.8 19.8 %collective-permute-start.2 = (f32[2,2,128,128]{3,2,1,0:T(8,128)S(1)}, f32[2,2,128,128]{3,2,1,0:T(8,128)S(1)}, u32[]{:S(2)}, u32[]{:S(2)}) collective-permute-start(f32[2,2,128,128]{3,2,1,0:T(8,128)S(1)} %get-tuple-element.20.refs_0_), channel_id=1, source_target_pairs={{0,8},{8,16},{16,24},{24,0},{4,28},{12,4},{20,12},{28,20},{1,9},{9... | collective-permute-start | bytes 786440 | tf_op jit(solution)/shard_map/ppermute | solution.py:253
  53.8 17.8 %collective-permute-start.5 = (f32[2,2,2,128,128]{4,3,2,1,0:T(8,128)S(1)}, f32[2,2,2,128,128]{4,3,2,1,0:T(8,128)S(1)}, u32[]{:S(2)}, u32[]{:S(2)}) collective-permute-start(f32[2,2,2,128,128]{4,3,2,1,0:T(8,128)S(1)} %collective-permute-done.4.refs_2_), channel_id=1, source_target_pairs={{0,8},{8,16},{16,24},{24,0},{4,28},{12,4},{20,12},{28,20},{1,9},{9... | collective-permute-start | bytes 1572872 | tf_op jit(solution)/shard_map/ppermute | solution.py:253
  53.9 17.7 %collective-permute-start.7 = (f32[2,2,2,128,128]{4,3,2,1,0:T(8,128)}, f32[2,2,2,128,128]{4,3,2,1,0:T(8,128)S(1)}, u32[]{:S(2)}, u32[]{:S(2)}) collective-permute-start(f32[2,2,2,128,128]{4,3,2,1,0:T(8,128)} %collective-permute-done.6.refs_4_), channel_id=1, source_target_pairs={{0,8},{8,16},{16,24},{24,0},{4,28},{12,4},{20,12},{28,20},{1,9},{9... | collective-permute-start | bytes 1572872 | tf_op jit(solution)/shard_map/ppermute | solution.py:253
  58.2 13.2 %collective-permute-start.10 = (f32[2,2,128,128]{3,2,1,0:T(8,128)S(1)}, f32[2,2,128,128]{3,2,1,0:T(8,128)S(1)}, u32[]{:S(2)}, u32[]{:S(2)}) collective-permute-start(f32[2,2,128,128]{3,2,1,0:T(8,128)S(1)} %slice_bitcast_fusion), channel_id=1, source_target_pairs={{0,32},{32,64},{64,96},{96,128},{128,160},{160,192},{192,224},{224... | collective-permute-start | bytes 786440 | tf_op jit(solution)/shard_map/ppermute | solution.py:253
  61.6 15.2 %collective-permute-start.9 = (f32[2,2,2,128,128]{4,3,2,1,0:T(8,128)S(1)}, f32[2,2,2,128,128]{4,3,2,1,0:T(8,128)S(1)}, u32[]{:S(2)}, u32[]{:S(2)}) collective-permute-start(f32[2,2,2,128,128]{4,3,2,1,0:T(8,128)S(1)} %collective-permute-done.8.refs_6_), channel_id=1, source_target_pairs={{0,8},{8,16},{16,24},{24,0},{4,28},{12,4},{20,12},{28,20},{1,9},{9... | collective-permute-start | bytes 1572872 | tf_op jit(solution)/shard_map/ppermute | solution.py:253
  63.3 1.6 %copy-start.1 = (f32[2,512,512]{2,1,0:T(8,128)S(1)}, f32[2,512,512]{2,1,0:T(8,128)}, u32[]{:S(2)}) copy-start(f32[2,512,512]{2,1,0:T(8,128)} %l_ref.1) | copy-start | bytes 6291460
  71.4 10.4 %copy-start = (f32[16,128,1,128]{3,2,1,0:T(1,128)S(1)}, f32[16,128,1,128]{3,2,1,0:T(1,128)}, u32[]{:S(2)}) copy-start(f32[16,128,1,128]{3,2,1,0:T(1,128)} %param.2) | copy-start | bytes 3145732
  71.4 5.4 %collective-permute-start.20 = (f32[2,2,128,128]{3,2,1,0:T(8,128)S(1)}, f32[2,2,128,128]{3,2,1,0:T(8,128)S(1)}, u32[]{:S(2)}, u32[]{:S(2)}) collective-permute-start(f32[2,2,128,128]{3,2,1,0:T(8,128)S(1)} %collective-permute-done.10.refs_8_), channel_id=1, source_target_pairs={{0,8},{8,16},{16,24},{24,0},{4,28},{12,4},{20,12},{28,20},{1,9},{9... | collective-permute-start | bytes 786440 | tf_op jit(solution)/shard_map/ppermute | solution.py:253
  79.8 2.0 %collective-permute-start.21 = (f32[1024,128]{1,0:T(8,128)S(1)}, f32[1024,128]{1,0:T(8,128)S(1)}, u32[]{:S(2)}, u32[]{:S(2)}) collective-permute-start(f32[1024,128]{1,0:T(8,128)S(1)} %get-tuple-element.18), channel_id=1, source_target_pairs={{0,4},{4,0},{1,5},{5,1},{2,6},{6,2},{3,7},{7,3},{8,12},{12,8},{9,1... | collective-permute-start | bytes 1572872 | tf_op jit(solution)/shard_map/ppermute | solution.py:20
